TPU v7x, 512 devices: a whole 4x8x8 slice. The times are simulated.
512 devices in a mesh: pair: 64 (over y, z), intg: 8 (over x, core).
Axes of the slice: x: 4, y: 8, z: 8, core: 2. Of those that a mesh axis runs over, the one named last changes fastest.
Arguments:
- amplitudes: bfloat16 [512, 128, 1024], P('pair'), may hold values from -6 to 6
- integrals: bfloat16 [2048, 128, 1024], P('intg', 'pair'), may hold values from -0.015625 to 0.015625
- tile_irreps: int32 [24], replicated, may hold values from 0 to 1
- screening: int32 [128], replicated, may hold values 0 or 1
- slot_tiles: int32 [128], replicated, may hold values from 0 to 127, each once
- pair_list: int32 [512, 2], P('pair'), may hold values from 0 to 299
- occupied_energy: float32 [300], replicated, may hold values from -1.2 to -0.3
- virtual_energy: float32 [768], replicated, may hold values from 0.2 to 1.5
Outputs:
- update: float32 [512, 2048], P('pair', 'intg')
Inputs may be any that keep to these rules, and one draw needn't show every extreme that they name: slot_tiles names every cd tile pair of the slab exactly once.
All inputs are finite; a program needn't handle non-finite values.
Results may differ from a plain program's by a relative error of at most 0.0003.
Values may be sent and summed in bfloat16 or wider, within the bound.
No kernel may reach another device: no remote copies, remote signals or barrier semaphores. Data moves between devices by JAX's collectives and lax.ppermute only.
A program may use at most 64 MiB of HBM per device.

v0:
```python
import jax
import jax.numpy as jnp
from jax import lax
from jax.sharding import PartitionSpec as P

TILE = 32
NT = 24


def lookup(table, index):
    places = jnp.arange(table.shape[0], dtype=jnp.int32)
    return jnp.sum(jnp.where(places[None, :] == index[:, None], table[None, :], 0), axis=1)


def on_device(
    amplitudes,
    integrals,
    tile_irreps,
    screening,
    slot_tiles,
    pair_list,
    occupied_energy,
    virtual_energy,
):
    slots_here = integrals.shape[1]
    ab_rows = integrals.shape[0]
    block = lax.axis_index("intg")
    owner = lax.axis_index("pair")
    first_tile = block // NT
    second_tile = block % NT
    sym_ab = jnp.bitwise_xor(
        lookup(tile_irreps, first_tile[None]), lookup(tile_irreps, second_tile[None])
    )
    my_slots = lax.dynamic_slice_in_dim(slot_tiles, owner * slots_here, slots_here)
    sym_cd = jnp.bitwise_xor(
        lookup(tile_irreps, my_slots // NT), lookup(tile_irreps, my_slots % NT)
    )
    keep = jnp.where(sym_cd == sym_ab, 1.0, 0.0).astype(jnp.float32) * lookup(
        screening, my_slots
    ).astype(jnp.float32)
    ordered = jnp.take(amplitudes, slot_tiles, axis=1)
    columns = lax.all_to_all(ordered, "pair", split_axis=1, concat_axis=0, tiled=True)
    masked_ints = integrals * keep.astype(jnp.bfloat16)[None, :, None]
    ladder = lax.psum_scatter(
        lax.dot_general(
            columns, masked_ints, (((1, 2), (1, 2)), ((), ())), preferred_element_type=jnp.float32
        ),
        "pair",
        scatter_dimension=0,
        tiled=True,
    )
    occupied_sum = lookup(occupied_energy, pair_list[:, 0]) + lookup(
        occupied_energy, pair_list[:, 1]
    )
    first_energy = lax.dynamic_slice_in_dim(virtual_energy, first_tile * TILE, TILE)
    second_energy = lax.dynamic_slice_in_dim(virtual_energy, second_tile * TILE, TILE)
    virtual_sum = jnp.repeat(first_energy[: ab_rows // TILE], TILE) + jnp.tile(
        second_energy, ab_rows // TILE
    )
    denom = occupied_sum[:, None] - virtual_sum[None, :]
    return ladder / denom


def solution(mesh):
    placed = (
        P("pair", None, None),
        P("intg", "pair", None),
        P(),
        P(),
        P(),
        P("pair", None),
        P(),
        P(),
    )
    return jax.shard_map(
        on_device, mesh=mesh, in_specs=placed, out_specs=P("pair", "intg"), check_vma=False
    )
```

profile of v0, /device:TPU:1, one launch (start us, length us, event | category | flops | bytes accessed | tf_op | source)
XLA Modules:
  0.0 253.1 jit_solution(17313821855280942886)
XLA Ops:
  6.5 0.0 copy-start
  6.5 0.8 compare_select_fusion
  7.3 0.7 compare_and_fusion
  8.0 0.1 copy-done
  8.1 8.1 %gather_fusion = bf16[128,8,1024]{2,0,1:T(8,128)(2,1)} fusion(bf16[8,128,1024]{2,1,0:T(8,128)(2,1)S(1)} %copy-done, s32[1024]{0:T(1024)S(1)} %pad_clamp_fusion), kind=kCustom, calls=%fused_computation | custom fusion | bytes 4194816 | tf_op jit(solution)/shard_map/jit(_take)/gather | solution.py:41
  16.2 1.8 select_bitcast_fusion
  18.0 2.4 copy.16
  20.5 0.0 copy-start.2
  20.5 0.0 copy-start.5
  20.5 0.0 copy-start.6
  20.5 0.0 copy-start.1
  20.5 17.5 %all-to-all-start = ((bf16[8,128,1024]{2,0,1:T(8,128)(2,1)}), bf16[8,128,1024]{2,0,1:T(8,128)(2,1)}, u32[]{:S(2)}, u32[]{:S(2)}) async-start(bf16[8,128,1024]{2,0,1:T(8,128)(2,1)} %copy.16), calls=%async_computation | async-start | bytes 4194304 | tf_op jit(solution)/shard_map/all_to_all | solution.py:42
  38.1 0.0 all-reduce.3.cloned.1.call-start
  38.1 0.0 copy-done.2
  38.2 0.6 fusion.11
  40.1 0.0 copy-done.5
  40.1 0.1 and_select_fusion.1
  40.2 0.8 fusion.14
  41.0 0.0 copy-done.6
  41.0 0.2 fusion.9
  41.2 0.2 fusion.8
  41.4 0.0 copy-done.1
  41.5 1.9 broadcast_multiply_fusion
  43.4 43.0 %all-to-all-done = bf16[8,128,1024]{2,0,1:T(8,128)(2,1)} async-done(((bf16[8,128,1024]{2,0,1:T(8,128)(2,1)}), bf16[8,128,1024]{2,0,1:T(8,128)(2,1)}, u32[]{:S(2)}, u32[]{:S(2)}) %all-to-all-start) | async-done | bytes 2097184 | tf_op jit(solution)/shard_map/all_to_all | solution.py:42
  86.4 0.0 copy-start.4
  86.4 0.0 copy-start.3
  86.4 3.4 %fusion.3 = f32[512,256]{1,0:T(8,128)} fusion(bf16[8,64,2,1024]{3,0,2,1:T(8,128)(2,1)} %bitcast.1, bf16[256,2,1024]{2,1,0:T(2,128)(2,1)} %broadcast_multiply_fusion), kind=kOutput, calls=%fused_computation.5 | convolution fusion | flops 536870912 | bytes 3670016 | tf_op jit(solution)/shard_map/dot_general | solution.py:45
  89.8 0.0 all-reduce.3.cloned.1.call-update
  89.8 0.1 broadcast_add_fusion
  89.9 0.1 add.57
  90.0 1.3 dynamic-slice
  91.9 0.0 copy-done.4
  91.9 0.0 copy-done.3
  91.9 0.2 select_reduce_fusion
  92.2 152.7 %all-reduce.3.cloned.1.call-done = f32[512,256]{1,0:T(8,128)} async-done(((f32[512,256]{1,0:T(8,128)}), f32[512,256]{1,0:T(8,128)}) %all-reduce.3.cloned.1.call-update) | async-done | bytes 524304
  244.8 1.4 dynamic-slice_divide_fusion
  (5 shorter events, 0.0 us)
Async XLA Ops:
  6.5 1.6 copy-start
  20.5 17.7 %copy-start.2 = (s32[24]{0:T(128)S(1)}, s32[24]{0:T(128)}, u32[]{:S(2)}) copy-start(s32[24]{0:T(128)} %param.10) | copy-start | bytes 292
  20.5 19.6 %copy-start.5 = (s32[128]{0:T(128)S(1)}, s32[128]{0:T(128)}, u32[]{:S(2)}) copy-start(s32[128]{0:T(128)} %param.12) | copy-start | bytes 1540
  20.5 20.5 %copy-start.6 = (s32[128]{0:T(128)S(1)}, s32[128]{0:T(128)}, u32[]{:S(2)}) copy-start(s32[128]{0:T(128)} %param.11) | copy-start | bytes 1540
  20.5 21.0 %copy-start.1 = (bf16[256,2,1024]{2,1,0:T(2,128)(2,1)S(1)}, bf16[256,2,1024]{2,1,0:T(2,128)(2,1)}, u32[]{:S(2)}) copy-start(bf16[256,2,1024]{2,1,0:T(2,128)(2,1)} %param.9) | copy-start | bytes 3145732
  20.5 65.9 %all-to-all-start = ((bf16[8,128,1024]{2,0,1:T(8,128)(2,1)}), bf16[8,128,1024]{2,0,1:T(8,128)(2,1)}, u32[]{:S(2)}, u32[]{:S(2)}) async-start(bf16[8,128,1024]{2,0,1:T(8,128)(2,1)} %copy.16), calls=%async_computation | async-start | bytes 4194304 | tf_op jit(solution)/shard_map/all_to_all | solution.py:42
  38.1 206.8 %all-reduce.3.cloned.1.call-start = ((), (), s32[]{:S(2)}) async-start(), calls=%async_computation.1 | async-start | bytes 1048576
  86.4 5.5 %copy-start.4 = (s32[8,2]{0,1:T(2,128)S(1)}, s32[8,2]{0,1:T(2,128)}, u32[]{:S(2)}) copy-start(s32[8,2]{0,1:T(2,128)} %param.13) | copy-start | bytes 196
  86.4 5.6 %copy-start.3 = (f32[300]{0:T(512)S(1)}, f32[300]{0:T(512)}, u32[]{:S(2)}) copy-start(f32[300]{0:T(512)} %param.14) | copy-start | bytes 3604
Sparse Core Ops, SparseCore 0:
  89.9 154.8 all-reduce.2
where the time goes:
time: 257 us; the launch traced here: 253 us
  waiting for transfers between devices  196 us (76%)
  starting transfers between devices  17.6 us (7%)
  between operations  15.5 us (6%)
  local copies, waits for them, and re-layouts  12.8 us (5%)
  other arithmetic  8.06 us (3%)
  matrix products  3.44 us (1%)
    unnamed x2, waiting for transfers between devices  153 us
    all_to_all x1, waiting for transfers between devices, on_device(): lax.all_to_all(ordered, 'pair', split_axis=1, concat_axis=0, tiled=True)  43 us
    all_to_all x1, starting transfers between devices, on_device(): lax.all_to_all(ordered, 'pair', split_axis=1, concat_axis=0, tiled=True)  17.5 us
    gather x1, local copies, waits for them, and re-layouts, on_device(): ordered = jnp.take(amplitudes, slot_tiles, axis=1)  8.06 us
  transfers between devices with their start and end apart: 2, of which 2 were waited for; matrix products, arithmetic and copies ran while one was open for 2% of the time, Pallas kernels for 0%

commit v1 on v0

--- a/solution.py
+++ b/solution.py
@@ -1,15 +1,94 @@
 import jax
 import jax.numpy as jnp
 from jax import lax
+from jax.experimental import pallas as pl
+from jax.experimental.pallas import tpu as pltpu
 from jax.sharding import PartitionSpec as P
 
 TILE = 32
 NT = 24
+CORES = 2
 
 
 def lookup(table, index):
     places = jnp.arange(table.shape[0], dtype=jnp.int32)
     return jnp.sum(jnp.where(places[None, :] == index[:, None], table[None, :], 0), axis=1)
+
+
+def pack_kernel(place, slot_ref, amp_ref, out_ref, rows):
+    owners, pairs, _ = rows.shape
+    tiles = amp_ref.shape[1]
+    slots = slot_ref.shape[1]
+    tile_at = lax.broadcasted_iota(jnp.int32, (tiles, slots), 0)
+    held = jnp.where(tile_at == slot_ref[...], 1.0, 0.0).astype(jnp.bfloat16)
+    owner_at = lax.broadcasted_iota(jnp.int32, (owners, slots), 0)
+    slot_at = lax.broadcasted_iota(jnp.int32, (owners, slots), 1)
+    mine = jnp.where(slot_at == owner_at * CORES + place[1], 1.0, 0.0).astype(jnp.bfloat16)
+    select = lax.dot_general(
+        mine, held, (((1,), (1,)), ((), ())), preferred_element_type=jnp.float32
+    ).astype(jnp.bfloat16)
+    for pair in range(pairs):
+        rows[:, pair, :] = jnp.dot(select, amp_ref[pair], preferred_element_type=jnp.float32)
+    out_ref[...] = rows[...].astype(jnp.bfloat16)
+
+
+def pack(place, slot_tiles, amplitudes, owners, width):
+    pairs, tiles, _ = amplitudes.shape
+    return pl.pallas_call(
+        pack_kernel,
+        out_shape=jax.ShapeDtypeStruct((owners, pairs, width), jnp.bfloat16),
+        grid_spec=pltpu.PrefetchScalarGridSpec(
+            num_scalar_prefetch=1,
+            grid=(1,),
+            in_specs=[
+                pl.BlockSpec((1, tiles), lambda k, place: (0, 0)),
+                pl.BlockSpec((pairs, tiles, width), lambda k, place: (0, 0, place[0])),
+            ],
+            out_specs=pl.BlockSpec((owners, pairs, width), lambda k, place: (0, 0, 0)),
+            scratch_shapes=[pltpu.VMEM((owners, pairs, width), jnp.float32)],
+        ),
+        compiler_params=pltpu.CompilerParams(vmem_limit_bytes=16 << 20),
+        name="pack",
+    )(place, slot_tiles[None, :], amplitudes)
+
+
+def ladder_kernel(place, own_ref, other_ref, mine_ref, theirs_ref, out_ref):
+    contract = (((1,), (1,)), ((), ()))
+    term = lax.dot_general(
+        own_ref[0], mine_ref[0], contract, preferred_element_type=jnp.float32
+    ) + lax.dot_general(
+        other_ref[0], theirs_ref[0], contract, preferred_element_type=jnp.float32
+    )
+
+    @pl.when(pl.program_id(0) == 0)
+    def _():
+        out_ref[...] = term
+
+    @pl.when(pl.program_id(0) > 0)
+    def _():
+        out_ref[...] += term
+
+
+def ladder_sums(place, own, other, ints):
+    quarters, rows, width = own.shape
+    cols = ints.shape[1]
+    return pl.pallas_call(
+        ladder_kernel,
+        out_shape=jax.ShapeDtypeStruct((rows, cols), jnp.float32),
+        grid_spec=pltpu.PrefetchScalarGridSpec(
+            num_scalar_prefetch=1,
+            grid=(quarters,),
+            in_specs=[
+                pl.BlockSpec((1, rows, width), lambda k, place: (k, 0, 0)),
+                pl.BlockSpec((1, rows, width), lambda k, place: (k, 0, 0)),
+                pl.BlockSpec((1, cols, width), lambda k, place: (place[1], 0, k)),
+                pl.BlockSpec((1, cols, width), lambda k, place: (1 - place[1], 0, k)),
+            ],
+            out_specs=pl.BlockSpec((rows, cols), lambda k, place: (0, 0)),
+        ),
+        compiler_params=pltpu.CompilerParams(vmem_limit_bytes=24 << 20),
+        name="ladder",
+    )(place, own, other, ints, ints)
 
 
 def on_device(
@@ -21,11 +100,22 @@
     pair_list,
     occupied_energy,
     virtual_energy,
+    n_pair,
+    n_intg,
 ):
+    pairs = amplitudes.shape[0]
     slots_here = integrals.shape[1]
     ab_rows = integrals.shape[0]
     block = lax.axis_index("intg")
     owner = lax.axis_index("pair")
+    quarters = n_intg // CORES
+    width = amplitudes.shape[2] // quarters
+    place = jnp.stack([block // CORES, block % CORES]).astype(jnp.int32)
+
+    send = pack(place, slot_tiles, amplitudes, n_pair, width)
+    piece = lax.all_to_all(send, "pair", split_axis=0, concat_axis=0, tiled=True)
+    piece = piece.reshape(n_pair * pairs, width)
+
     first_tile = block // NT
     second_tile = block % NT
     sym_ab = jnp.bitwise_xor(
@@ -38,17 +128,24 @@
     keep = jnp.where(sym_cd == sym_ab, 1.0, 0.0).astype(jnp.float32) * lookup(
         screening, my_slots
     ).astype(jnp.float32)
-    ordered = jnp.take(amplitudes, slot_tiles, axis=1)
-    columns = lax.all_to_all(ordered, "pair", split_axis=1, concat_axis=0, tiled=True)
-    masked_ints = integrals * keep.astype(jnp.bfloat16)[None, :, None]
-    ladder = lax.psum_scatter(
-        lax.dot_general(
-            columns, masked_ints, (((1, 2), (1, 2)), ((), ())), preferred_element_type=jnp.float32
-        ),
-        "pair",
-        scatter_dimension=0,
+    masked_ints = jnp.transpose(integrals * keep.astype(jnp.bfloat16)[None, :, None], (1, 0, 2))
+
+    same_core = [list(range(core, n_intg, CORES)) for core in range(CORES)]
+    own = lax.all_to_all(
+        jnp.broadcast_to(piece[None], (quarters,) + piece.shape),
+        "intg",
+        split_axis=0,
+        concat_axis=0,
         tiled=True,
+        axis_index_groups=same_core,
     )
+    other = lax.ppermute(own, "intg", [(i, i ^ 1) for i in range(n_intg)])
+    partial = ladder_sums(place, own, other, masked_ints)
+    parts = lax.all_to_all(
+        partial.reshape(n_pair, pairs, ab_rows), "pair", split_axis=0, concat_axis=0, tiled=True
+    )
+    ladder = jnp.sum(parts, axis=0)
+
     occupied_sum = lookup(occupied_energy, pair_list[:, 0]) + lookup(
         occupied_energy, pair_list[:, 1]
     )
@@ -72,6 +169,11 @@
         P(),
         P(),
     )
+    n_pair, n_intg = mesh.shape["pair"], mesh.shape["intg"]
+
+    def part(*arrays):
+        return on_device(*arrays, n_pair, n_intg)
+
     return jax.shard_map(
-        on_device, mesh=mesh, in_specs=placed, out_specs=P("pair", "intg"), check_vma=False
+        part, mesh=mesh, in_specs=placed, out_specs=P("pair", "intg"), check_vma=False
     )

time: 257 us -> 87.1 us (0.34)
  the two profiles are of different devices: /device:TPU:1 before, /device:TPU:16 now
where the time goes in v1:
time: 87.1 us; the launch traced here: 86.7 us
  waiting for transfers between devices  31.8 us (37%)
  blocking collectives  30.3 us (35%)
  starting transfers between devices  12.1 us (14%)
  local copies, waits for them, and re-layouts  4.27 us (5%)
  Pallas kernels  4.06 us (5%)
  other arithmetic  2.68 us (3%)
  between operations  1.49 us (2%)
    all_to_all x1, blocking collectives, on_device(): lax.all_to_all(send, 'pair', split_axis=0, concat_axis=0, tiled=True)  30.3 us
    all_to_all x1, waiting for transfers between devices, on_device(): lax.all_to_all(partial.reshape(n_pair, pairs, ab_rows), 'pair', split_axi...  18.4 us
    all_to_all x1, waiting for transfers between devices, on_device(): lax.all_to_all(jnp.broadcast_to(piece[None], (quarters,) + piece.shape),...  11.7 us
    all_to_all x1, starting transfers between devices, on_device(): lax.all_to_all(partial.reshape(n_pair, pairs, ab_rows), 'pair', split_axi...  5.87 us
    all_to_all x1, starting transfers between devices, on_device(): lax.all_to_all(jnp.broadcast_to(piece[None], (quarters,) + piece.shape),...  4.29 us
    pallas_call x1, Pallas kernels, ladder_sums(): pl.pallas_call(ladder_kernel, out_shape=jax.ShapeDtypeStruct((rows, cols)...  3.07 us
    unnamed x16, local copies, waits for them, and re-layouts  2.28 us
    ppermute x1, starting transfers between devices, on_device(): other = lax.ppermute(own, 'intg', [(i, i ^ 1) for i in range(n_intg)])  1.91 us
  transfers between devices with their start and end apart: 3, of which 3 were waited for; matrix products, arithmetic and copies ran while one was open for 3% of the time, Pallas kernels for 0%

profile of v1, /device:TPU:16, one launch (start us, length us, event | category | flops | bytes accessed | tf_op | source)
XLA Modules:
  0.0 86.7 jit_solution(1207853885186526779)
XLA Ops:
  0.0 0.1 pad_add_fusion.place
  0.1 0.0 copy-start
  0.1 1.6 %copy-done = bf16[8,128,1024]{2,1,0:T(8,128)(2,1)S(1)} copy-done((bf16[8,128,1024]{2,1,0:T(8,128)(2,1)S(1)}, bf16[8,128,1024]{2,1,0:T(8,128)(2,1)}, u32[]{:S(2)}) %copy-start) | copy-done | bytes 2097176
  1.7 0.0 copy-start.1
  1.7 0.7 copy-done.1
  2.3 1.0 %pack.1 = bf16[64,8,256]{2,1,0:T(8,128)(2,1)S(1)} custom-call(s32[2]{0:T(128)S(1)} %pad_add_fusion.place, s32[1,128]{1,0:T(1,128)S(1)} %bitcast.12, bf16[8,128,1024]{2,1,0:T(8,128)(2,1)S(1)} %copy-done), custom_call_target="tpu_custom_call" | custom-call | tf_op jit(solution)/shard_map/pack/pallas_call | solution.py:37
  3.3 0.0 copy-start.4
  3.3 0.0 copy-start.2
  3.4 0.0 copy-start.7
  3.4 0.0 copy-start.3
  3.4 30.3 %all_to_all.15 = bf16[64,8,256]{2,1,0:T(8,128)(2,1)S(1)} all-to-all(bf16[64,8,256]{2,1,0:T(8,128)(2,1)S(1)} %pack.1), channel_id=1, replica_groups=mesh['pair'=64,'intg'=8] {'pair'}, dimensions={0} | all-to-all | bytes 524288 | tf_op jit(solution)/shard_map/all_to_all | solution.py:116
  33.7 1.1 %broadcast_in_dim.92 = bf16[4,512,256]{2,1,0:T(8,128)(2,1)} broadcast(bf16[512,256]{1,0:T(8,128)(2,1)S(1)} %bitcast.13), dimensions={1,2} | broadcast | bytes 1310720 | tf_op jit(solution)/shard_map/broadcast_in_dim | solution.py:135
  34.8 4.3 %all-to-all-start.1 = ((bf16[4,512,256]{2,1,0:T(8,128)(2,1)}), bf16[4,512,256]{2,1,0:T(8,128)(2,1)S(1)}, u32[]{:S(2)}, u32[]{:S(2)}) async-start(bf16[4,512,256]{2,1,0:T(8,128)(2,1)} %broadcast_in_dim.92), calls=%async_computation.1 | async-start | bytes 2097152 | tf_op jit(solution)/shard_map/all_to_all | solution.py:134
  39.1 0.0 copy-done.4
  39.1 0.7 fusion.5
  41.1 11.7 %all-to-all-done.1.own_ref = bf16[4,512,256]{2,1,0:T(8,128)(2,1)S(1)} async-done(((bf16[4,512,256]{2,1,0:T(8,128)(2,1)}), bf16[4,512,256]{2,1,0:T(8,128)(2,1)S(1)}, u32[]{:S(2)}, u32[]{:S(2)}) %all-to-all-start.1) | async-done | bytes 1048608 | tf_op jit(solution)/shard_map/all_to_all | solution.py:134
  52.8 1.9 %collective-permute-start = (bf16[4,512,256]{2,1,0:T(8,128)(2,1)S(1)}, bf16[4,512,256]{2,1,0:T(8,128)(2,1)S(1)}, u32[]{:S(2)}, u32[]{:S(2)}) collective-permute-start(bf16[4,512,256]{2,1,0:T(8,128)(2,1)S(1)} %all-to-all-done.1.own_ref), channel_id=1, source_target_pairs={{0,1},{1,0},{2,3},{3,2},{4,5},{5,4},{6,7},{7,6},{8,9},{9,8},{10,11... | collective-permute-start | bytes 3145736 | tf_op jit(solution)/shard_map/ppermute | solution.py:142
  54.7 0.0 copy-done.2
  54.7 0.1 and_select_fusion.1
  54.8 0.0 copy-done.7
  54.8 0.2 fusion.3
  55.0 0.2 fusion.2
  55.2 0.0 copy-done.3
  55.3 0.3 fusion.mine_ref.theirs_ref
  55.6 0.0 copy-start.6
  55.6 0.0 copy-start.5
  55.6 1.7 %collective-permute-done.other_ref = bf16[4,512,256]{2,1,0:T(8,128)(2,1)S(1)} collective-permute-done((bf16[4,512,256]{2,1,0:T(8,128)(2,1)S(1)}, bf16[4,512,256]{2,1,0:T(8,128)(2,1)S(1)}, u32[]{:S(2)}, u32[]{:S(2)}) %collective-permute-start) | collective-permute-done | bytes 1048608 | tf_op jit(solution)/shard_map/ppermute | solution.py:142
  57.3 3.1 %ladder.1 = f32[512,256]{1,0:T(8,128)} custom-call(s32[2]{0:T(128)S(1)} %pad_add_fusion.place, bf16[4,512,256]{2,1,0:T(8,128)(2,1)S(1)} %all-to-all-done.1.own_ref, bf16[4,512,256]{2,1,0:T(8,128)(2,1)S(1)} %collective-permute-done.other_ref, bf16[2,256,1024]{2,1,0:T(8,128)(2,1)S(1)} %fusion.mine_ref.theirs_ref, bf16[2,256,1024]{2,1,0:T(8,128)(2,1)S(1)} %fusion.mine_ref.theirs_ref), custom_call_target="tpu_custom_call" | custom-call | tf_op jit(solution)/shard_map/ladder/pallas_call | solution.py:75
  60.4 5.9 %all-to-all-start.2 = ((f32[64,8,256]{2,1,0:T(8,128)}), f32[64,8,256]{2,1,0:T(8,128)S(1)}, u32[]{:S(2)}, u32[]{:S(2)}) async-start(f32[64,8,256]{2,1,0:T(8,128)} %bitcast.5), calls=%async_computation.2 | async-start | bytes 1048576 | tf_op jit(solution)/shard_map/all_to_all | solution.py:144
  66.3 0.8 fusion.8
  67.1 0.1 broadcast_add_fusion
  67.2 0.1 add.50
  67.3 0.0 copy-done.6
  67.3 0.0 copy-done.5
  67.3 0.2 select_reduce_fusion
  67.5 18.4 %all-to-all-done.2 = f32[64,8,256]{2,1,0:T(8,128)S(1)} async-done(((f32[64,8,256]{2,1,0:T(8,128)}), f32[64,8,256]{2,1,0:T(8,128)S(1)}, u32[]{:S(2)}, u32[]{:S(2)}) %all-to-all-start.2) | async-done | bytes 524320 | tf_op jit(solution)/shard_map/all_to_all | solution.py:144
  86.0 0.1 reduce_sum.77
  86.1 0.7 subtract_divide_fusion
  (4 shorter events, 0.0 us)
Async XLA Ops:
  0.1 1.6 %copy-start = (bf16[8,128,1024]{2,1,0:T(8,128)(2,1)S(1)}, bf16[8,128,1024]{2,1,0:T(8,128)(2,1)}, u32[]{:S(2)}) copy-start(bf16[8,128,1024]{2,1,0:T(8,128)(2,1)} %amp_ref.1) | copy-start | bytes 6291460
  1.7 0.7 copy-start.1
  3.3 35.7 %copy-start.4 = (s32[24]{0:T(128)S(1)}, s32[24]{0:T(128)}, u32[]{:S(2)}) copy-start(s32[24]{0:T(128)} %param.10) | copy-start | bytes 292
  3.3 51.4 %copy-start.2 = (s32[128]{0:T(128)S(1)}, s32[128]{0:T(128)}, u32[]{:S(2)}) copy-start(s32[128]{0:T(128)} %param.12) | copy-start | bytes 1540
  3.4 51.5 %copy-start.7 = (s32[128]{0:T(128)S(1)}, s32[128]{0:T(128)}, u32[]{:S(2)}) copy-start(s32[128]{0:T(128)} %param.11) | copy-start | bytes 1540
  3.4 51.9 %copy-start.3 = (bf16[256,2,1024]{2,1,0:T(2,128)(2,1)S(1)}, bf16[256,2,1024]{2,1,0:T(2,128)(2,1)}, u32[]{:S(2)}) copy-start(bf16[256,2,1024]{2,1,0:T(2,128)(2,1)} %param.9) | copy-start | bytes 3145732
  34.8 18.0 %all-to-all-start.1 = ((bf16[4,512,256]{2,1,0:T(8,128)(2,1)}), bf16[4,512,256]{2,1,0:T(8,128)(2,1)S(1)}, u32[]{:S(2)}, u32[]{:S(2)}) async-start(bf16[4,512,256]{2,1,0:T(8,128)(2,1)} %broadcast_in_dim.92), calls=%async_computation.1 | async-start | bytes 2097152 | tf_op jit(solution)/shard_map/all_to_all | solution.py:134
  52.8 4.5 %collective-permute-start = (bf16[4,512,256]{2,1,0:T(8,128)(2,1)S(1)}, bf16[4,512,256]{2,1,0:T(8,128)(2,1)S(1)}, u32[]{:S(2)}, u32[]{:S(2)}) collective-permute-start(bf16[4,512,256]{2,1,0:T(8,128)(2,1)S(1)} %all-to-all-done.1.own_ref), channel_id=1, source_target_pairs={{0,1},{1,0},{2,3},{3,2},{4,5},{5,4},{6,7},{7,6},{8,9},{9,8},{10,11... | collective-permute-start | bytes 3145736 | tf_op jit(solution)/shard_map/ppermute | solution.py:142
  55.6 11.7 %copy-start.6 = (s32[8,2]{0,1:T(2,128)S(1)}, s32[8,2]{0,1:T(2,128)}, u32[]{:S(2)}) copy-start(s32[8,2]{0,1:T(2,128)} %param.13) | copy-start | bytes 196
  55.6 11.7 %copy-start.5 = (f32[300]{0:T(512)S(1)}, f32[300]{0:T(512)}, u32[]{:S(2)}) copy-start(f32[300]{0:T(512)} %param.14) | copy-start | bytes 3604
  60.4 25.6 %all-to-all-start.2 = ((f32[64,8,256]{2,1,0:T(8,128)}), f32[64,8,256]{2,1,0:T(8,128)S(1)}, u32[]{:S(2)}, u32[]{:S(2)}) async-start(f32[64,8,256]{2,1,0:T(8,128)} %bitcast.5), calls=%async_computation.2 | async-start | bytes 1048576 | tf_op jit(solution)/shard_map/all_to_all | solution.py:144

commit v2 on v0

--- a/solution.py
+++ b/solution.py
@@ -1,15 +1,115 @@
+import functools
+
 import jax
 import jax.numpy as jnp
 from jax import lax
+from jax.experimental import pallas as pl
+from jax.experimental.pallas import tpu as pltpu
 from jax.sharding import PartitionSpec as P
 
 TILE = 32
 NT = 24
+CORES = 2
+SLOTS = 2
 
 
 def lookup(table, index):
     places = jnp.arange(table.shape[0], dtype=jnp.int32)
     return jnp.sum(jnp.where(places[None, :] == index[:, None], table[None, :], 0), axis=1)
+
+
+def pack_kernel(slot_ref, amp_ref, out_ref, slots_in, amp_in, rows, slot_sem, amp_sems):
+    owners, _, width = rows.shape
+    steps, half, tiles, _ = amp_in.shape
+    slots = slots_in.shape[1]
+    core = lax.axis_index("intg") % CORES
+    slot_copy = pltpu.make_async_copy(slot_ref, slots_in, slot_sem)
+    slot_copy.start()
+    amp_copies = [
+        pltpu.make_async_copy(
+            amp_ref.at[pl.ds(core * half, half), :, pl.ds(step * width, width)],
+            amp_in.at[step],
+            amp_sems.at[step],
+        )
+        for step in range(steps)
+    ]
+    for copy in amp_copies:
+        copy.start()
+    tile_at = lax.broadcasted_iota(jnp.int32, (tiles, slots), 0)
+    owner_at = lax.broadcasted_iota(jnp.int32, (owners, slots), 0)
+    slot_at = lax.broadcasted_iota(jnp.int32, (owners, slots), 1)
+    slot_copy.wait()
+    held = jnp.where(tile_at == slots_in[...], 1.0, 0.0).astype(jnp.bfloat16)
+    select = []
+    for slot in range(SLOTS):
+        mine = jnp.where(slot_at == owner_at * SLOTS + slot, 1.0, 0.0).astype(jnp.bfloat16)
+        select.append(
+            lax.dot_general(
+                mine, held, (((1,), (1,)), ((), ())), preferred_element_type=jnp.float32
+            ).astype(jnp.bfloat16)
+        )
+    select = jnp.concatenate(select)
+    for step, copy in enumerate(amp_copies):
+        copy.wait()
+        for j in range(half):
+            picked = jnp.dot(select, amp_in[step, j], preferred_element_type=jnp.float32)
+            for slot in range(SLOTS):
+                rows[:, slot * half + j, :] = picked[slot * owners : (slot + 1) * owners]
+        out_ref[:, :, step * width : (step + 1) * width] = rows[...].astype(jnp.bfloat16)
+
+
+def pack(slot_tiles, amplitudes, owners):
+    pairs, tiles, entries = amplitudes.shape
+    half = pairs // CORES
+    width = min(256, entries)
+    steps = entries // width
+    return pl.pallas_call(
+        pack_kernel,
+        out_shape=jax.ShapeDtypeStruct((owners, SLOTS * half, entries), jnp.bfloat16),
+        in_specs=[pl.BlockSpec(memory_space=pltpu.HBM)] * 2,
+        out_specs=pl.BlockSpec(memory_space=pltpu.VMEM),
+        scratch_shapes=[
+            pltpu.VMEM((1, slot_tiles.shape[0]), jnp.int32),
+            pltpu.VMEM((steps, half, tiles, width), jnp.bfloat16),
+            pltpu.VMEM((owners, SLOTS * half, width), jnp.float32),
+            pltpu.SemaphoreType.DMA,
+            pltpu.SemaphoreType.DMA((steps,)),
+        ],
+        compiler_params=pltpu.CompilerParams(vmem_limit_bytes=16 << 20),
+        name="pack",
+    )(
+        pltpu.with_memory_space_constraint(slot_tiles[None, :], pltpu.HBM),
+        pltpu.with_memory_space_constraint(amplitudes, pltpu.HBM),
+    )
+
+
+def ladder_kernel(half, mine_ref, theirs_ref, columns_ref, out_ref):
+    columns = columns_ref[...]
+
+    def product(ints_ref, slot):
+        return lax.dot_general(
+            columns,
+            ints_ref[slot],
+            (((1,), (1,)), ((), ())),
+            preferred_element_type=jnp.float32,
+        ).reshape(out_ref.shape)
+
+    first = lax.broadcasted_iota(jnp.int32, out_ref.shape, 1) < half
+    kept = jnp.where(first, product(mine_ref, 0), product(theirs_ref, 1))
+    moved = jnp.where(first, product(theirs_ref, 0), product(mine_ref, 1))
+    out_ref[...] = kept + pltpu.roll(moved, half, 1)
+
+
+def ladder_sums(owners, half, mine, theirs, columns):
+    cols = mine.shape[1]
+    return pl.pallas_call(
+        functools.partial(ladder_kernel, half),
+        out_shape=jax.ShapeDtypeStruct((owners, CORES * half, cols), jnp.float32),
+        in_specs=[pl.BlockSpec(memory_space=pltpu.VMEM)] * 3,
+        out_specs=pl.BlockSpec(memory_space=pltpu.VMEM),
+        compiler_params=pltpu.CompilerParams(vmem_limit_bytes=24 << 20),
+        name="ladder",
+    )(mine, theirs, columns)
 
 
 def on_device(
@@ -21,11 +121,23 @@
     pair_list,
     occupied_energy,
     virtual_energy,
+    n_pair,
+    n_intg,
 ):
+    pairs = amplitudes.shape[0]
     slots_here = integrals.shape[1]
     ab_rows = integrals.shape[0]
     block = lax.axis_index("intg")
     owner = lax.axis_index("pair")
+    half = pairs // CORES
+    swap = [(i, i ^ 1) for i in range(n_intg)]
+
+    send, integrals = lax.optimization_barrier(
+        (pack(slot_tiles, amplitudes, n_pair), integrals)
+    )
+    columns = lax.all_to_all(send, "pair", split_axis=0, concat_axis=0, tiled=True)
+    columns = columns.reshape(n_pair * SLOTS * half, amplitudes.shape[2])
+
     first_tile = block // NT
     second_tile = block % NT
     sym_ab = jnp.bitwise_xor(
@@ -38,17 +150,18 @@
     keep = jnp.where(sym_cd == sym_ab, 1.0, 0.0).astype(jnp.float32) * lookup(
         screening, my_slots
     ).astype(jnp.float32)
-    ordered = jnp.take(amplitudes, slot_tiles, axis=1)
-    columns = lax.all_to_all(ordered, "pair", split_axis=1, concat_axis=0, tiled=True)
-    masked_ints = integrals * keep.astype(jnp.bfloat16)[None, :, None]
-    ladder = lax.psum_scatter(
-        lax.dot_general(
-            columns, masked_ints, (((1, 2), (1, 2)), ((), ())), preferred_element_type=jnp.float32
-        ),
-        "pair",
-        scatter_dimension=0,
-        tiled=True,
+    masked_ints = jnp.transpose(integrals * keep.astype(jnp.bfloat16)[None, :, None], (1, 0, 2))
+
+    other_ints = lax.ppermute(masked_ints, "intg", swap)
+    partial = ladder_sums(n_pair, half, masked_ints, other_ints, columns)
+    parts = lax.all_to_all(partial, "pair", split_axis=0, concat_axis=0, tiled=True)
+    halves = jnp.sum(parts, axis=0)
+    kept = halves[:half]
+    came = lax.ppermute(halves[half:], "intg", swap)
+    ladder = jnp.where(
+        block % CORES == 0, jnp.concatenate([kept, came]), jnp.concatenate([came, kept])
     )
+
     occupied_sum = lookup(occupied_energy, pair_list[:, 0]) + lookup(
         occupied_energy, pair_list[:, 1]
     )
@@ -72,6 +185,11 @@
         P(),
         P(),
     )
+    n_pair, n_intg = mesh.shape["pair"], mesh.shape["intg"]
+
+    def part(*arrays):
+        return on_device(*arrays, n_pair, n_intg)
+
     return jax.shard_map(
-        on_device, mesh=mesh, in_specs=placed, out_specs=P("pair", "intg"), check_vma=False
+        part, mesh=mesh, in_specs=placed, out_specs=P("pair", "intg"), check_vma=False
     )

time: 257 us -> 82.6 us (0.32); the launches traced: 253 us -> 82.1 us
  waiting for transfers between devices: 196 us -> 36.7 us
  starting transfers between devices: 17.6 us -> 34.8 us
  between operations: 15.5 us -> 1.52 us
  local copies, waits for them, and re-layouts: 12.8 us -> 0.95 us
  Pallas kernels: 0 us -> 5.53 us
  other arithmetic: 8.06 us -> 2.6 us
  matrix products: 3.44 us -> 0 us
    unnamed x2 -> x0, waiting for transfers between devices: 153 us -> none
    all_to_all x1 -> x2, waiting for transfers between devices: 43 us -> 34 us  [the longest x1 18.6 us: on_device(): lax.all_to_all(send, 'pair', split_axis=0, concat_axis=0, tiled=True)]
    ppermute x0 -> x2, starting transfers between devices: none -> 8.67 us  [the longest x1 5.8 us: on_device(): came = lax.ppermute(halves[half:], 'intg', swap)]
    all_to_all x1 -> x2, starting transfers between devices: 17.5 us -> 26.2 us  [the longest x1 17.1 us: on_device(): lax.all_to_all(send, 'pair', split_axis=0, concat_axis=0, tiled=True)]
    gather x1 -> x0, local copies, waits for them, and re-layouts: 8.06 us -> none  [on_device(): ordered = jnp.take(amplitudes, slot_tiles, axis=1)]
    pallas_call x0 -> x2, Pallas kernels: none -> 5.53 us  [the longest x1 3.45 us: pack(): pl.pallas_call(pack_kernel, out_shape=jax.ShapeDtypeStruct((owners, SLOTS...]
    dot_general x1 -> x0, matrix products: 3.44 us -> none  [on_device(): lax.dot_general(columns, masked_ints, (((1, 2), (1, 2)), ((), ())), prefe...]
    ppermute x0 -> x2, waiting for transfers between devices: none -> 2.75 us  [the longest x1 2.26 us: on_device(): other_ints = lax.ppermute(masked_ints, 'intg', swap)]
  transfers between devices with their start and end apart: 2 -> 4, of which waited for: 2 -> 4; matrix products, arithmetic and copies ran while one was open for 2% -> 3% of each run, Pallas kernels for 0% -> 0%
where the time goes in v2:
time: 82.6 us; the launch traced here: 82.1 us
  waiting for transfers between devices  36.7 us (44%)
  starting transfers between devices  34.8 us (42%)
  Pallas kernels  5.53 us (7%)
  other arithmetic  2.6 us (3%)
  between operations  1.52 us (2%)
  local copies, waits for them, and re-layouts  0.95 us (1%)
    all_to_all x1, waiting for transfers between devices, on_device(): lax.all_to_all(send, 'pair', split_axis=0, concat_axis=0, tiled=True)  18.6 us
    all_to_all x1, starting transfers between devices, on_device(): lax.all_to_all(send, 'pair', split_axis=0, concat_axis=0, tiled=True)  17.1 us
    all_to_all x1, waiting for transfers between devices, on_device(): lax.all_to_all(partial, 'pair', split_axis=0, concat_axis=0, tiled=True)  15.4 us
    all_to_all x1, starting transfers between devices, on_device(): lax.all_to_all(partial, 'pair', split_axis=0, concat_axis=0, tiled=True)  9.02 us
    ppermute x1, starting transfers between devices, on_device(): came = lax.ppermute(halves[half:], 'intg', swap)  5.8 us
    pallas_call x1, Pallas kernels, pack(): pl.pallas_call(pack_kernel, out_shape=jax.ShapeDtypeStruct((owners, SLOTS...  3.45 us
    ppermute x1, starting transfers between devices, on_device(): other_ints = lax.ppermute(masked_ints, 'intg', swap)  2.86 us
    ppermute x1, waiting for transfers between devices, on_device(): other_ints = lax.ppermute(masked_ints, 'intg', swap)  2.26 us
  transfers between devices with their start and end apart: 4, of which 4 were waited for; matrix products, arithmetic and copies ran while one was open for 3% of the time, Pallas kernels for 0%

profile of v2, /device:TPU:1, one launch (start us, length us, event | category | flops | bytes accessed | tf_op | source)
XLA Modules:
  0.0 82.1 jit_solution(4078750346147291301)
XLA Ops:
  0.0 0.0 copy-start.1
  0.0 0.0 copy-start.3
  0.0 0.0 copy-start.5
  0.0 0.0 copy-start
  0.0 3.5 %pack.1 = bf16[64,8,1024]{2,1,0:T(8,128)(2,1)} custom-call(s32[1,128]{1,0:T(1,128)} %bitcast.11, bf16[8,128,1024]{2,1,0:T(8,128)(2,1)} %amp_ref.1), custom_call_target="tpu_custom_call" | custom-call | tf_op jit(solution)/shard_map/pack/pallas_call | solution.py:66
  3.5 17.1 %all-to-all-start = ((bf16[64,8,1024]{2,1,0:T(8,128)(2,1)}), bf16[64,8,1024]{2,1,0:T(8,128)(2,1)S(1)}, u32[]{:S(2)}, u32[]{:S(2)}) async-start(bf16[64,8,1024]{2,1,0:T(8,128)(2,1)} %pack.1), calls=%async_computation | async-start | bytes 2097152 | tf_op jit(solution)/shard_map/all_to_all | solution.py:138
  20.7 0.0 copy-done.1
  20.7 0.7 fusion.6
  22.7 0.0 copy-done.3
  22.7 0.1 and_select_fusion.1
  22.8 0.0 copy-done.5
  22.8 0.2 fusion.4
  23.0 0.2 fusion.3
  23.3 0.0 copy-done
  23.3 0.3 fusion.mine_ref
  23.6 2.9 %collective-permute-start = (bf16[2,256,1024]{2,1,0:T(8,128)(2,1)S(1)}, bf16[2,256,1024]{2,1,0:T(8,128)(2,1)S(1)}, u32[]{:S(2)}, u32[]{:S(2)}) collective-permute-start(bf16[2,256,1024]{2,1,0:T(8,128)(2,1)S(1)} %fusion.mine_ref), channel_id=1, source_target_pairs={{0,1},{1,0},{2,3},{3,2},{4,5},{5,4},{6,7},{7,6},{8,9},{9,8},{10,11... | collective-permute-start | bytes 3145736 | tf_op jit(solution)/shard_map/ppermute | solution.py:155
  26.5 2.3 %collective-permute-done.theirs_ref = bf16[2,256,1024]{2,1,0:T(8,128)(2,1)S(1)} collective-permute-done((bf16[2,256,1024]{2,1,0:T(8,128)(2,1)S(1)}, bf16[2,256,1024]{2,1,0:T(8,128)(2,1)S(1)}, u32[]{:S(2)}, u32[]{:S(2)}) %collective-permute-start) | collective-permute-done | bytes 1048608 | tf_op jit(solution)/shard_map/ppermute | solution.py:155
  28.8 18.6 %all-to-all-done = bf16[64,8,1024]{2,1,0:T(8,128)(2,1)S(1)} async-done(((bf16[64,8,1024]{2,1,0:T(8,128)(2,1)}), bf16[64,8,1024]{2,1,0:T(8,128)(2,1)S(1)}, u32[]{:S(2)}, u32[]{:S(2)}) %all-to-all-start) | async-done | bytes 1048608 | tf_op jit(solution)/shard_map/all_to_all | solution.py:138
  47.4 0.0 copy-start.4
  47.4 0.0 copy-start.2
  47.4 2.1 %ladder.1 = f32[64,8,256]{2,1,0:T(8,128)} custom-call(bf16[2,256,1024]{2,1,0:T(8,128)(2,1)S(1)} %fusion.mine_ref, bf16[2,256,1024]{2,1,0:T(8,128)(2,1)S(1)} %collective-permute-done.theirs_ref, bf16[512,1024]{1,0:T(8,128)(2,1)S(1)} %bitcast.9), custom_call_target="tpu_custom_call" | custom-call | tf_op jit(solution)/shard_map/ladder/pallas_call | solution.py:105
  49.4 9.0 %all-to-all-start.1 = ((f32[64,8,256]{2,1,0:T(8,128)}), f32[64,8,256]{2,1,0:T(8,128)S(1)}, u32[]{:S(2)}, u32[]{:S(2)}) async-start(f32[64,8,256]{2,1,0:T(8,128)} %ladder.1), calls=%async_computation.1 | async-start | bytes 1048576 | tf_op jit(solution)/shard_map/all_to_all | solution.py:157
  58.5 0.8 %fusion.10 = (f32[32]{0:T(128)S(1)}, f32[32]{0:T(128)S(1)}) fusion(f32[768]{0:T(1024)} %param.15, s32[]{:T(128)S(6)} %select_n.94, s32[]{:T(128)S(6)} %select_n.95), kind=kLoop, calls=%fused_computation.27 | loop fusion | bytes 520 | tf_op jit(solution)/shard_map/dynamic_slice | solution.py:168
  59.3 0.0 copy-done.4
  59.3 0.1 broadcast_add_fusion
  59.4 15.4 %all-to-all-done.1 = f32[64,8,256]{2,1,0:T(8,128)S(1)} async-done(((f32[64,8,256]{2,1,0:T(8,128)}), f32[64,8,256]{2,1,0:T(8,128)S(1)}, u32[]{:S(2)}, u32[]{:S(2)}) %all-to-all-start.1) | async-done | bytes 524320 | tf_op jit(solution)/shard_map/all_to_all | solution.py:157
  74.8 0.1 reduce_sum.77
  74.9 5.8 %collective-permute-start.1 = (f32[4,256]{1,0:T(4,128)S(1)}, f32[4,256]{1,0:T(4,128)S(1)}, u32[]{:S(2)}, u32[]{:S(2)}) collective-permute-start(f32[4,256]{1,0:T(4,128)S(1)} %get-tuple-element.18), channel_id=1, source_target_pairs={{0,1},{1,0},{2,3},{3,2},{4,5},{5,4},{6,7},{7,6},{8,9},{9,8},{10,11... | collective-permute-start | bytes 12296 | tf_op jit(solution)/shard_map/ppermute | solution.py:160
  80.7 0.0 copy-done.2
  80.7 0.2 select_reduce_fusion
  80.9 0.1 add.49
  81.0 0.5 collective-permute-done.1
  81.5 0.7 fusion.1
  (5 shorter events, 0.0 us)
Async XLA Ops:
  0.0 20.7 %copy-start.1 = (s32[24]{0:T(128)S(1)}, s32[24]{0:T(128)}, u32[]{:S(2)}) copy-start(s32[24]{0:T(128)} %param.10) | copy-start | bytes 292
  0.0 22.7 %copy-start.3 = (s32[128]{0:T(128)S(1)}, s32[128]{0:T(128)}, u32[]{:S(2)}) copy-start(s32[128]{0:T(128)} %param.12) | copy-start | bytes 1540
  0.0 22.8 %copy-start.5 = (s32[128]{0:T(128)S(1)}, s32[128]{0:T(128)}, u32[]{:S(2)}) copy-start(s32[128]{0:T(128)} %param.11) | copy-start | bytes 1540
  0.0 23.3 %copy-start = (bf16[256,2,1024]{2,1,0:T(2,128)(2,1)S(1)}, bf16[256,2,1024]{2,1,0:T(2,128)(2,1)}, u32[]{:S(2)}) copy-start(bf16[256,2,1024]{2,1,0:T(2,128)(2,1)} %param.9) | copy-start | bytes 3145732
  3.5 43.9 %all-to-all-start = ((bf16[64,8,1024]{2,1,0:T(8,128)(2,1)}), bf16[64,8,1024]{2,1,0:T(8,128)(2,1)S(1)}, u32[]{:S(2)}, u32[]{:S(2)}) async-start(bf16[64,8,1024]{2,1,0:T(8,128)(2,1)} %pack.1), calls=%async_computation | async-start | bytes 2097152 | tf_op jit(solution)/shard_map/all_to_all | solution.py:138
  23.6 5.1 %collective-permute-start = (bf16[2,256,1024]{2,1,0:T(8,128)(2,1)S(1)}, bf16[2,256,1024]{2,1,0:T(8,128)(2,1)S(1)}, u32[]{:S(2)}, u32[]{:S(2)}) collective-permute-start(bf16[2,256,1024]{2,1,0:T(8,128)(2,1)S(1)} %fusion.mine_ref), channel_id=1, source_target_pairs={{0,1},{1,0},{2,3},{3,2},{4,5},{5,4},{6,7},{7,6},{8,9},{9,8},{10,11... | collective-permute-start | bytes 3145736 | tf_op jit(solution)/shard_map/ppermute | solution.py:155
  47.4 12.0 %copy-start.4 = (s32[8,2]{0,1:T(2,128)S(1)}, s32[8,2]{0,1:T(2,128)}, u32[]{:S(2)}) copy-start(s32[8,2]{0,1:T(2,128)} %param.13) | copy-start | bytes 196
  47.4 33.3 %copy-start.2 = (f32[300]{0:T(512)S(1)}, f32[300]{0:T(512)}, u32[]{:S(2)}) copy-start(f32[300]{0:T(512)} %param.14) | copy-start | bytes 3604
  49.4 25.3 %all-to-all-start.1 = ((f32[64,8,256]{2,1,0:T(8,128)}), f32[64,8,256]{2,1,0:T(8,128)S(1)}, u32[]{:S(2)}, u32[]{:S(2)}) async-start(f32[64,8,256]{2,1,0:T(8,128)} %ladder.1), calls=%async_computation.1 | async-start | bytes 1048576 | tf_op jit(solution)/shard_map/all_to_all | solution.py:157
  74.9 6.6 %collective-permute-start.1 = (f32[4,256]{1,0:T(4,128)S(1)}, f32[4,256]{1,0:T(4,128)S(1)}, u32[]{:S(2)}, u32[]{:S(2)}) collective-permute-start(f32[4,256]{1,0:T(4,128)S(1)} %get-tuple-element.18), channel_id=1, source_target_pairs={{0,1},{1,0},{2,3},{3,2},{4,5},{5,4},{6,7},{7,6},{8,9},{9,8},{10,11... | collective-permute-start | bytes 12296 | tf_op jit(solution)/shard_map/ppermute | solution.py:160

commit v3 on v2

--- a/solution.py
+++ b/solution.py
@@ -11,6 +11,7 @@
 NT = 24
 CORES = 2
 SLOTS = 2
+SHARES = 2
 
 
 def lookup(table, index):
@@ -18,23 +19,22 @@
     return jnp.sum(jnp.where(places[None, :] == index[:, None], table[None, :], 0), axis=1)
 
 
-def pack_kernel(slot_ref, amp_ref, out_ref, slots_in, amp_in, rows, slot_sem, amp_sems):
+def pack_kernel(slot_ref, amp_ref, out_ref, slots_in, amp_in, rows, slot_sem, amp_sem):
     owners, _, width = rows.shape
-    steps, half, tiles, _ = amp_in.shape
+    half, tiles, _ = amp_in.shape
     slots = slots_in.shape[1]
-    core = lax.axis_index("intg") % CORES
+    place = lax.axis_index("intg")
+    share, core = place // CORES % SHARES, place % CORES
     slot_copy = pltpu.make_async_copy(slot_ref, slots_in, slot_sem)
+    amp_copy = pltpu.make_async_copy(
+        amp_ref.at[
+            pl.ds(core * half, half), :, pl.ds(pl.multiple_of(share * width, width), width)
+        ],
+        amp_in,
+        amp_sem,
+    )
     slot_copy.start()
-    amp_copies = [
-        pltpu.make_async_copy(
-            amp_ref.at[pl.ds(core * half, half), :, pl.ds(step * width, width)],
-            amp_in.at[step],
-            amp_sems.at[step],
-        )
-        for step in range(steps)
-    ]
-    for copy in amp_copies:
-        copy.start()
+    amp_copy.start()
     tile_at = lax.broadcasted_iota(jnp.int32, (tiles, slots), 0)
     owner_at = lax.broadcasted_iota(jnp.int32, (owners, slots), 0)
     slot_at = lax.broadcasted_iota(jnp.int32, (owners, slots), 1)
@@ -49,31 +49,28 @@
             ).astype(jnp.bfloat16)
         )
     select = jnp.concatenate(select)
-    for step, copy in enumerate(amp_copies):
-        copy.wait()
-        for j in range(half):
-            picked = jnp.dot(select, amp_in[step, j], preferred_element_type=jnp.float32)
-            for slot in range(SLOTS):
-                rows[:, slot * half + j, :] = picked[slot * owners : (slot + 1) * owners]
-        out_ref[:, :, step * width : (step + 1) * width] = rows[...].astype(jnp.bfloat16)
-
-
-def pack(slot_tiles, amplitudes, owners):
-    pairs, tiles, entries = amplitudes.shape
+    amp_copy.wait()
+    for j in range(half):
+        picked = jnp.dot(select, amp_in[j], preferred_element_type=jnp.float32)
+        for slot in range(SLOTS):
+            rows[:, slot * half + j, :] = picked[slot * owners : (slot + 1) * owners]
+    out_ref[...] = rows[...].astype(jnp.bfloat16)
+
+
+def pack(slot_tiles, amplitudes, owners, width):
+    pairs, tiles, _ = amplitudes.shape
     half = pairs // CORES
-    width = min(256, entries)
-    steps = entries // width
     return pl.pallas_call(
         pack_kernel,
-        out_shape=jax.ShapeDtypeStruct((owners, SLOTS * half, entries), jnp.bfloat16),
+        out_shape=jax.ShapeDtypeStruct((owners, SLOTS * half, width), jnp.bfloat16),
         in_specs=[pl.BlockSpec(memory_space=pltpu.HBM)] * 2,
         out_specs=pl.BlockSpec(memory_space=pltpu.VMEM),
         scratch_shapes=[
             pltpu.VMEM((1, slot_tiles.shape[0]), jnp.int32),
-            pltpu.VMEM((steps, half, tiles, width), jnp.bfloat16),
+            pltpu.VMEM((half, tiles, width), jnp.bfloat16),
             pltpu.VMEM((owners, SLOTS * half, width), jnp.float32),
             pltpu.SemaphoreType.DMA,
-            pltpu.SemaphoreType.DMA((steps,)),
+            pltpu.SemaphoreType.DMA,
         ],
         compiler_params=pltpu.CompilerParams(vmem_limit_bytes=16 << 20),
         name="pack",
@@ -83,16 +80,22 @@
     )
 
 
-def ladder_kernel(half, mine_ref, theirs_ref, columns_ref, out_ref):
-    columns = columns_ref[...]
+def ladder_kernel(half, mine_ref, theirs_ref, piece_ref, other_ref, out_ref):
+    width = piece_ref.shape[1]
+    share = lax.axis_index("intg") // CORES % SHARES
+    here = pl.ds(pl.multiple_of(share * width, width), width)
+    there = pl.ds(pl.multiple_of((1 - share) * width, width), width)
+
+    def dot(rows, ints):
+        return lax.dot_general(
+            rows, ints, (((1,), (1,)), ((), ())), preferred_element_type=jnp.float32
+        )
 
     def product(ints_ref, slot):
-        return lax.dot_general(
-            columns,
-            ints_ref[slot],
-            (((1,), (1,)), ((), ())),
-            preferred_element_type=jnp.float32,
-        ).reshape(out_ref.shape)
+        total = dot(piece_ref[...], ints_ref[slot, :, here]) + dot(
+            other_ref[...], ints_ref[slot, :, there]
+        )
+        return total.reshape(out_ref.shape)
 
     first = lax.broadcasted_iota(jnp.int32, out_ref.shape, 1) < half
     kept = jnp.where(first, product(mine_ref, 0), product(theirs_ref, 1))
@@ -100,16 +103,16 @@
     out_ref[...] = kept + pltpu.roll(moved, half, 1)
 
 
-def ladder_sums(owners, half, mine, theirs, columns):
+def ladder_sums(owners, half, mine, theirs, piece, other):
     cols = mine.shape[1]
     return pl.pallas_call(
         functools.partial(ladder_kernel, half),
         out_shape=jax.ShapeDtypeStruct((owners, CORES * half, cols), jnp.float32),
-        in_specs=[pl.BlockSpec(memory_space=pltpu.VMEM)] * 3,
+        in_specs=[pl.BlockSpec(memory_space=pltpu.VMEM)] * 4,
         out_specs=pl.BlockSpec(memory_space=pltpu.VMEM),
         compiler_params=pltpu.CompilerParams(vmem_limit_bytes=24 << 20),
         name="ladder",
-    )(mine, theirs, columns)
+    )(mine, theirs, piece, other)
 
 
 def on_device(
@@ -129,14 +132,13 @@
     ab_rows = integrals.shape[0]
     block = lax.axis_index("intg")
     owner = lax.axis_index("pair")
-    half = pairs // CORES
-    swap = [(i, i ^ 1) for i in range(n_intg)]
+    width = amplitudes.shape[2] // SHARES
 
     send, integrals = lax.optimization_barrier(
-        (pack(slot_tiles, amplitudes, n_pair), integrals)
-    )
-    columns = lax.all_to_all(send, "pair", split_axis=0, concat_axis=0, tiled=True)
-    columns = columns.reshape(n_pair * SLOTS * half, amplitudes.shape[2])
+        (pack(slot_tiles, amplitudes, n_pair, width), integrals)
+    )
+    piece = lax.all_to_all(send, "pair", split_axis=0, concat_axis=0, tiled=True)
+    piece = piece.reshape(n_pair * pairs, width)
 
     first_tile = block // NT
     second_tile = block % NT
@@ -152,8 +154,13 @@
     ).astype(jnp.float32)
     masked_ints = jnp.transpose(integrals * keep.astype(jnp.bfloat16)[None, :, None], (1, 0, 2))
 
+    swap = [(i, i ^ 1) for i in range(n_intg)]
     other_ints = lax.ppermute(masked_ints, "intg", swap)
-    partial = ladder_sums(n_pair, half, masked_ints, other_ints, columns)
+
+    ring = [(i, (i + (CORES if i % CORES == 0 else -CORES)) % n_intg) for i in range(n_intg)]
+    other = lax.ppermute(piece, "intg", ring)
+    half = pairs // CORES
+    partial = ladder_sums(n_pair, half, masked_ints, other_ints, piece, other)
     parts = lax.all_to_all(partial, "pair", split_axis=0, concat_axis=0, tiled=True)
     halves = jnp.sum(parts, axis=0)
     kept = halves[:half]

time: 82.6 us -> 81 us (0.981)
  waiting for transfers between devices: 36.7 us -> 30.7 us
  starting transfers between devices: 34.8 us -> 40.3 us
  Pallas kernels: 5.53 us -> 4.53 us
    all_to_all x1, waiting for transfers between devices: 18.6 us -> 10.5 us  [on_device(): lax.all_to_all(send, 'pair', split_axis=0, concat_axis=0, tiled=True)]
    ppermute x0 -> x1, waiting for transfers between devices: none -> 6.09 us  [on_device(): other = lax.ppermute(piece, 'intg', ring)]
    ppermute x0 -> x1, starting transfers between devices: none -> 4.51 us  [on_device(): other = lax.ppermute(piece, 'intg', ring)]
    ppermute x1, waiting for transfers between devices: 2.26 us -> 0.01 us  [on_device(): other_ints = lax.ppermute(masked_ints, 'intg', swap)]
    ppermute x1, starting transfers between devices: 5.8 us -> 7.94 us  [on_device(): came = lax.ppermute(halves[half:], 'intg', swap)]
    all_to_all x1, waiting for transfers between devices: 15.4 us -> 13.6 us  [on_device(): lax.all_to_all(partial, 'pair', split_axis=0, concat_axis=0, tiled=True)]
    all_to_all x1, starting transfers between devices: 9.02 us -> 7.8 us  [on_device(): lax.all_to_all(partial, 'pair', split_axis=0, concat_axis=0, tiled=True)]
    pallas_call x1, Pallas kernels: 3.45 us -> 2.45 us  [pack(): pl.pallas_call(pack_kernel, out_shape=jax.ShapeDtypeStruct((owners, SLOTS...]
  transfers between devices with their start and end apart: 4 -> 5, of which waited for: 4 -> 4; matrix products, arithmetic and copies ran while one was open for 3% -> 3% of each run, Pallas kernels for 0% -> 0%
where the time goes in v3:
time: 81 us; the launch traced here: 80.6 us
  starting transfers between devices  40.3 us (50%)
  waiting for transfers between devices  30.7 us (38%)
  Pallas kernels  4.53 us (6%)
  other arithmetic  2.61 us (3%)
  between operations  1.54 us (2%)
  local copies, waits for them, and re-layouts  0.95 us (1%)
    all_to_all x1, starting transfers between devices, on_device(): lax.all_to_all(send, 'pair', split_axis=0, concat_axis=0, tiled=True)  17.1 us
    all_to_all x1, waiting for transfers between devices, on_device(): lax.all_to_all(partial, 'pair', split_axis=0, concat_axis=0, tiled=True)  13.6 us
    all_to_all x1, waiting for transfers between devices, on_device(): lax.all_to_all(send, 'pair', split_axis=0, concat_axis=0, tiled=True)  10.5 us
    ppermute x1, starting transfers between devices, on_device(): came = lax.ppermute(halves[half:], 'intg', swap)  7.94 us
    all_to_all x1, starting transfers between devices, on_device(): lax.all_to_all(partial, 'pair', split_axis=0, concat_axis=0, tiled=True)  7.8 us
    ppermute x1, waiting for transfers between devices, on_device(): other = lax.ppermute(piece, 'intg', ring)  6.09 us
    ppermute x1, starting transfers between devices, on_device(): other = lax.ppermute(piece, 'intg', ring)  4.51 us
    ppermute x1, starting transfers between devices, on_device(): other_ints = lax.ppermute(masked_ints, 'intg', swap)  2.86 us
  transfers between devices with their start and end apart: 5, of which 4 were waited for; matrix products, arithmetic and copies ran while one was open for 3% of the time, Pallas kernels for 0%

profile of v3, /device:TPU:1, one launch (start us, length us, event | category | flops | bytes accessed | tf_op | source)
XLA Modules:
  0.0 80.6 jit_solution(5651626460586621123)
XLA Ops:
  0.0 0.0 copy-start.3
  0.0 0.0 copy-start
  0.0 0.0 copy-start.5
  0.0 0.0 copy-start.1
  0.0 2.5 %pack.1 = bf16[64,8,512]{2,1,0:T(8,128)(2,1)} custom-call(s32[1,128]{1,0:T(1,128)} %bitcast.12, bf16[8,128,1024]{2,1,0:T(8,128)(2,1)} %amp_ref.1), custom_call_target="tpu_custom_call" | custom-call | tf_op jit(solution)/shard_map/pack/pallas_call | solution.py:63
  2.5 17.1 %all-to-all-start = ((bf16[64,8,512]{2,1,0:T(8,128)(2,1)}), bf16[64,8,512]{2,1,0:T(8,128)(2,1)S(1)}, u32[]{:S(2)}, u32[]{:S(2)}) async-start(bf16[64,8,512]{2,1,0:T(8,128)(2,1)} %pack.1), calls=%async_computation | async-start | bytes 1048576 | tf_op jit(solution)/shard_map/all_to_all | solution.py:140
  19.7 0.0 copy-done.3
  19.7 0.1 and_select_fusion.1
  19.8 0.0 copy-done.5
  19.8 0.2 fusion.4
  20.0 0.0 copy-done.1
  20.0 0.2 fusion.3
  20.2 0.7 fusion.6
  22.3 0.0 copy-done
  22.3 0.3 fusion.mine_ref
  22.6 2.9 %collective-permute-start = (bf16[2,256,1024]{2,1,0:T(8,128)(2,1)S(1)}, bf16[2,256,1024]{2,1,0:T(8,128)(2,1)S(1)}, u32[]{:S(2)}, u32[]{:S(2)}) collective-permute-start(bf16[2,256,1024]{2,1,0:T(8,128)(2,1)S(1)} %fusion.mine_ref), channel_id=1, source_target_pairs={{0,1},{1,0},{2,3},{3,2},{4,5},{5,4},{6,7},{7,6},{8,9},{9,8},{10,11... | collective-permute-start | bytes 3145736 | tf_op jit(solution)/shard_map/ppermute | solution.py:158
  25.5 10.5 %all-to-all-done = bf16[64,8,512]{2,1,0:T(8,128)(2,1)S(1)} async-done(((bf16[64,8,512]{2,1,0:T(8,128)(2,1)}), bf16[64,8,512]{2,1,0:T(8,128)(2,1)S(1)}, u32[]{:S(2)}, u32[]{:S(2)}) %all-to-all-start) | async-done | bytes 524320 | tf_op jit(solution)/shard_map/all_to_all | solution.py:140
  36.0 0.0 copy-start.4
  36.0 0.0 copy-start.2
  36.0 4.5 %collective-permute-start.1 = (bf16[512,512]{1,0:T(8,128)(2,1)S(1)}, bf16[512,512]{1,0:T(8,128)(2,1)S(1)}, u32[]{:S(2)}, u32[]{:S(2)}) collective-permute-start(bf16[512,512]{1,0:T(8,128)(2,1)S(1)} %bitcast.9), channel_id=1, source_target_pairs={{0,2},{1,7},{2,4},{3,1},{4,6},{5,3},{6,0},{7,5},{8,10},{9,15},{10,... | collective-permute-start | bytes 1572872 | tf_op jit(solution)/shard_map/ppermute | solution.py:161
  40.5 0.0 collective-permute-done.theirs_ref
  40.5 6.1 %collective-permute-done.1.other_ref = bf16[512,512]{1,0:T(8,128)(2,1)S(1)} collective-permute-done((bf16[512,512]{1,0:T(8,128)(2,1)S(1)}, bf16[512,512]{1,0:T(8,128)(2,1)S(1)}, u32[]{:S(2)}, u32[]{:S(2)}) %collective-permute-start.1) | collective-permute-done | bytes 524320 | tf_op jit(solution)/shard_map/ppermute | solution.py:161
  46.6 2.1 %ladder.1 = f32[64,8,256]{2,1,0:T(8,128)} custom-call(bf16[2,256,1024]{2,1,0:T(8,128)(2,1)S(1)} %fusion.mine_ref, bf16[2,256,1024]{2,1,0:T(8,128)(2,1)S(1)} %collective-permute-done.theirs_ref, bf16[512,512]{1,0:T(8,128)(2,1)S(1)} %bitcast.10, bf16[512,512]{1,0:T(8,128)(2,1)S(1)} %collective-permute-done.1.other_ref), custom_call_target="tpu_custom_call" | custom-call | tf_op jit(solution)/shard_map/ladder/pallas_call | solution.py:108
  48.7 7.8 %all-to-all-start.1 = ((f32[64,8,256]{2,1,0:T(8,128)}), f32[64,8,256]{2,1,0:T(8,128)S(1)}, u32[]{:S(2)}, u32[]{:S(2)}) async-start(f32[64,8,256]{2,1,0:T(8,128)} %ladder.1), calls=%async_computation.1 | async-start | bytes 1048576 | tf_op jit(solution)/shard_map/all_to_all | solution.py:164
  56.5 0.8 %fusion.10 = (f32[32]{0:T(128)S(1)}, f32[32]{0:T(128)S(1)}) fusion(f32[768]{0:T(1024)} %param.15, s32[]{:T(128)S(6)} %select_n.94, s32[]{:T(128)S(6)} %select_n.95), kind=kLoop, calls=%fused_computation.27 | loop fusion | bytes 520 | tf_op jit(solution)/shard_map/dynamic_slice | solution.py:175
  57.4 0.0 copy-done.4
  57.4 0.1 broadcast_add_fusion
  57.4 13.6 %all-to-all-done.1 = f32[64,8,256]{2,1,0:T(8,128)S(1)} async-done(((f32[64,8,256]{2,1,0:T(8,128)}), f32[64,8,256]{2,1,0:T(8,128)S(1)}, u32[]{:S(2)}, u32[]{:S(2)}) %all-to-all-start.1) | async-done | bytes 524320 | tf_op jit(solution)/shard_map/all_to_all | solution.py:164
  71.0 0.1 reduce_sum.77
  71.1 7.9 %collective-permute-start.2 = (f32[4,256]{1,0:T(4,128)S(1)}, f32[4,256]{1,0:T(4,128)S(1)}, u32[]{:S(2)}, u32[]{:S(2)}) collective-permute-start(f32[4,256]{1,0:T(4,128)S(1)} %get-tuple-element.18), channel_id=1, source_target_pairs={{0,1},{1,0},{2,3},{3,2},{4,5},{5,4},{6,7},{7,6},{8,9},{9,8},{10,11... | collective-permute-start | bytes 12296 | tf_op jit(solution)/shard_map/ppermute | solution.py:167
  79.1 0.0 copy-done.2
  79.1 0.2 select_reduce_fusion
  79.3 0.1 add.49
  79.4 0.5 collective-permute-done.2
  79.9 0.7 fusion.1
  (5 shorter events, 0.0 us)
Async XLA Ops:
  0.0 19.7 %copy-start.3 = (s32[128]{0:T(128)S(1)}, s32[128]{0:T(128)}, u32[]{:S(2)}) copy-start(s32[128]{0:T(128)} %param.12) | copy-start | bytes 1540
  0.0 22.3 %copy-start = (bf16[256,2,1024]{2,1,0:T(2,128)(2,1)S(1)}, bf16[256,2,1024]{2,1,0:T(2,128)(2,1)}, u32[]{:S(2)}) copy-start(bf16[256,2,1024]{2,1,0:T(2,128)(2,1)} %param.9) | copy-start | bytes 3145732
  0.0 19.8 %copy-start.5 = (s32[128]{0:T(128)S(1)}, s32[128]{0:T(128)}, u32[]{:S(2)}) copy-start(s32[128]{0:T(128)} %param.11) | copy-start | bytes 1540
  0.0 20.0 %copy-start.1 = (s32[24]{0:T(128)S(1)}, s32[24]{0:T(128)}, u32[]{:S(2)}) copy-start(s32[24]{0:T(128)} %param.10) | copy-start | bytes 292
  2.5 33.5 %all-to-all-start = ((bf16[64,8,512]{2,1,0:T(8,128)(2,1)}), bf16[64,8,512]{2,1,0:T(8,128)(2,1)S(1)}, u32[]{:S(2)}, u32[]{:S(2)}) async-start(bf16[64,8,512]{2,1,0:T(8,128)(2,1)} %pack.1), calls=%async_computation | async-start | bytes 1048576 | tf_op jit(solution)/shard_map/all_to_all | solution.py:140
  22.6 17.9 %collective-permute-start = (bf16[2,256,1024]{2,1,0:T(8,128)(2,1)S(1)}, bf16[2,256,1024]{2,1,0:T(8,128)(2,1)S(1)}, u32[]{:S(2)}, u32[]{:S(2)}) collective-permute-start(bf16[2,256,1024]{2,1,0:T(8,128)(2,1)S(1)} %fusion.mine_ref), channel_id=1, source_target_pairs={{0,1},{1,0},{2,3},{3,2},{4,5},{5,4},{6,7},{7,6},{8,9},{9,8},{10,11... | collective-permute-start | bytes 3145736 | tf_op jit(solution)/shard_map/ppermute | solution.py:158
  36.0 21.4 %copy-start.4 = (s32[8,2]{0,1:T(2,128)S(1)}, s32[8,2]{0,1:T(2,128)}, u32[]{:S(2)}) copy-start(s32[8,2]{0,1:T(2,128)} %param.13) | copy-start | bytes 196
  36.0 43.1 %copy-start.2 = (f32[300]{0:T(512)S(1)}, f32[300]{0:T(512)}, u32[]{:S(2)}) copy-start(f32[300]{0:T(512)} %param.14) | copy-start | bytes 3604
  36.0 10.6 %collective-permute-start.1 = (bf16[512,512]{1,0:T(8,128)(2,1)S(1)}, bf16[512,512]{1,0:T(8,128)(2,1)S(1)}, u32[]{:S(2)}, u32[]{:S(2)}) collective-permute-start(bf16[512,512]{1,0:T(8,128)(2,1)S(1)} %bitcast.9), channel_id=1, source_target_pairs={{0,2},{1,7},{2,4},{3,1},{4,6},{5,3},{6,0},{7,5},{8,10},{9,15},{10,... | collective-permute-start | bytes 1572872 | tf_op jit(solution)/shard_map/ppermute | solution.py:161
  48.7 22.4 %all-to-all-start.1 = ((f32[64,8,256]{2,1,0:T(8,128)}), f32[64,8,256]{2,1,0:T(8,128)S(1)}, u32[]{:S(2)}, u32[]{:S(2)}) async-start(f32[64,8,256]{2,1,0:T(8,128)} %ladder.1), calls=%async_computation.1 | async-start | bytes 1048576 | tf_op jit(solution)/shard_map/all_to_all | solution.py:164
  71.1 8.7 %collective-permute-start.2 = (f32[4,256]{1,0:T(4,128)S(1)}, f32[4,256]{1,0:T(4,128)S(1)}, u32[]{:S(2)}, u32[]{:S(2)}) collective-permute-start(f32[4,256]{1,0:T(4,128)S(1)} %get-tuple-element.18), channel_id=1, source_target_pairs={{0,1},{1,0},{2,3},{3,2},{4,5},{5,4},{6,7},{7,6},{8,9},{9,8},{10,11... | collective-permute-start | bytes 12296 | tf_op jit(solution)/shard_map/ppermute | solution.py:167

commit v4 on v3

--- a/solution.py
+++ b/solution.py
@@ -17,6 +17,10 @@
 def lookup(table, index):
     places = jnp.arange(table.shape[0], dtype=jnp.int32)
     return jnp.sum(jnp.where(places[None, :] == index[:, None], table[None, :], 0), axis=1)
+
+
+def owner_in_turn(owners, place):
+    return (place + owners // 2 + owners // 16) % owners
 
 
 def pack_kernel(slot_ref, amp_ref, out_ref, slots_in, amp_in, rows, slot_sem, amp_sem):
@@ -36,7 +40,7 @@
     slot_copy.start()
     amp_copy.start()
     tile_at = lax.broadcasted_iota(jnp.int32, (tiles, slots), 0)
-    owner_at = lax.broadcasted_iota(jnp.int32, (owners, slots), 0)
+    owner_at = owner_in_turn(owners, lax.broadcasted_iota(jnp.int32, (owners, slots), 0))
     slot_at = lax.broadcasted_iota(jnp.int32, (owners, slots), 1)
     slot_copy.wait()
     held = jnp.where(tile_at == slots_in[...], 1.0, 0.0).astype(jnp.bfloat16)
@@ -134,10 +138,11 @@
     owner = lax.axis_index("pair")
     width = amplitudes.shape[2] // SHARES
 
+    in_turn = [[owner_in_turn(n_pair, place) for place in range(n_pair)]]
     send, integrals = lax.optimization_barrier(
         (pack(slot_tiles, amplitudes, n_pair, width), integrals)
     )
-    piece = lax.all_to_all(send, "pair", split_axis=0, concat_axis=0, tiled=True)
+    piece = lax.all_to_all(send, "pair", split_axis=0, concat_axis=0, tiled=True, axis_index_groups=in_turn)
     piece = piece.reshape(n_pair * pairs, width)
 
     first_tile = block // NT
@@ -161,7 +166,7 @@
     other = lax.ppermute(piece, "intg", ring)
     half = pairs // CORES
     partial = ladder_sums(n_pair, half, masked_ints, other_ints, piece, other)
-    parts = lax.all_to_all(partial, "pair", split_axis=0, concat_axis=0, tiled=True)
+    parts = lax.all_to_all(partial, "pair", split_axis=0, concat_axis=0, tiled=True, axis_index_groups=in_turn)
     halves = jnp.sum(parts, axis=0)
     kept = halves[:half]
     came = lax.ppermute(halves[half:], "intg", swap)

time: 81 us -> 76.4 us (0.943)
  waiting for transfers between devices: 30.7 us -> 21.4 us
  starting transfers between devices: 40.3 us -> 45 us
    all_to_all x2, waiting for transfers between devices: 24.1 us -> 14.8 us  [the longest x1 9.39 us: on_device(): lax.all_to_all(partial, 'pair', split_axis=0, concat_axis=0, tiled=True,...]
    all_to_all x2, starting transfers between devices: 24.9 us -> 32.6 us  [the longest x1 20.1 us: on_device(): lax.all_to_all(send, 'pair', split_axis=0, concat_axis=0, tiled=True, axi...]
    ppermute x1, starting transfers between devices: 7.94 us -> 4.69 us  [on_device(): came = lax.ppermute(halves[half:], 'intg', swap)]
  transfers between devices with their start and end apart: 5 -> 5, of which waited for: 4 -> 4; matrix products, arithmetic and copies ran while one was open for 3% -> 4% of each run, Pallas kernels for 0% -> 0%
where the time goes in v4:
time: 76.4 us; the launch traced here: 76 us
  starting transfers between devices  45 us (59%)
  waiting for transfers between devices  21.4 us (28%)
  Pallas kernels  4.53 us (6%)
  other arithmetic  2.61 us (3%)
  between operations  1.54 us (2%)
  local copies, waits for them, and re-layouts  0.95 us (1%)
    all_to_all x1, starting transfers between devices, on_device(): lax.all_to_all(send, 'pair', split_axis=0, concat_axis=0, tiled=True, axi...  20.1 us
    all_to_all x1, starting transfers between devices, on_device(): lax.all_to_all(partial, 'pair', split_axis=0, concat_axis=0, tiled=True,...  12.6 us
    all_to_all x1, waiting for transfers between devices, on_device(): lax.all_to_all(partial, 'pair', split_axis=0, concat_axis=0, tiled=True,...  9.39 us
    ppermute x1, waiting for transfers between devices, on_device(): other = lax.ppermute(piece, 'intg', ring)  6.09 us
    all_to_all x1, waiting for transfers between devices, on_device(): lax.all_to_all(send, 'pair', split_axis=0, concat_axis=0, tiled=True, axi...  5.37 us
    ppermute x1, starting transfers between devices, on_device(): came = lax.ppermute(halves[half:], 'intg', swap)  4.69 us
    ppermute x1, starting transfers between devices, on_device(): other = lax.ppermute(piece, 'intg', ring)  4.5 us
    ppermute x1, starting transfers between devices, on_device(): other_ints = lax.ppermute(masked_ints, 'intg', swap)  3.14 us
  transfers between devices with their start and end apart: 5, of which 4 were waited for; matrix products, arithmetic and copies ran while one was open for 4% of the time, Pallas kernels for 0%

profile of v4, /device:TPU:1, one launch (start us, length us, event | category | flops | bytes accessed | tf_op | source)
XLA Modules:
  0.0 76.0 jit_solution(3359264498559719549)
XLA Ops:
  0.0 0.0 copy-start.3
  0.0 0.0 copy-start
  0.0 0.0 copy-start.5
  0.0 0.0 copy-start.1
  0.0 2.5 %pack.1 = bf16[64,8,512]{2,1,0:T(8,128)(2,1)} custom-call(s32[1,128]{1,0:T(1,128)} %bitcast.12, bf16[8,128,1024]{2,1,0:T(8,128)(2,1)} %amp_ref.1), custom_call_target="tpu_custom_call" | custom-call | tf_op jit(solution)/shard_map/pack/pallas_call | solution.py:67
  2.5 20.1 %all-to-all-start = ((bf16[64,8,512]{2,1,0:T(8,128)(2,1)}), bf16[64,8,512]{2,1,0:T(8,128)(2,1)S(1)}, u32[]{:S(2)}, u32[]{:S(2)}) async-start(bf16[64,8,512]{2,1,0:T(8,128)(2,1)} %pack.1), calls=%async_computation | async-start | bytes 1048576 | tf_op jit(solution)/shard_map/all_to_all | solution.py:145
  22.6 0.0 copy-done.3
  22.6 0.1 and_select_fusion.1
  22.7 0.0 copy-done.5
  22.7 0.2 fusion.4
  22.9 0.0 copy-done.1
  22.9 0.2 fusion.3
  23.1 0.7 fusion.6
  25.2 0.0 copy-done
  25.2 0.3 fusion.mine_ref
  25.6 3.1 %collective-permute-start = (bf16[2,256,1024]{2,1,0:T(8,128)(2,1)S(1)}, bf16[2,256,1024]{2,1,0:T(8,128)(2,1)S(1)}, u32[]{:S(2)}, u32[]{:S(2)}) collective-permute-start(bf16[2,256,1024]{2,1,0:T(8,128)(2,1)S(1)} %fusion.mine_ref), channel_id=1, source_target_pairs={{0,1},{1,0},{2,3},{3,2},{4,5},{5,4},{6,7},{7,6},{8,9},{9,8},{10,11... | collective-permute-start | bytes 3145736 | tf_op jit(solution)/shard_map/ppermute | solution.py:163
  28.7 5.4 %all-to-all-done = bf16[64,8,512]{2,1,0:T(8,128)(2,1)S(1)} async-done(((bf16[64,8,512]{2,1,0:T(8,128)(2,1)}), bf16[64,8,512]{2,1,0:T(8,128)(2,1)S(1)}, u32[]{:S(2)}, u32[]{:S(2)}) %all-to-all-start) | async-done | bytes 524320 | tf_op jit(solution)/shard_map/all_to_all | solution.py:145
  34.1 0.0 copy-start.4
  34.1 0.0 copy-start.2
  34.1 4.5 %collective-permute-start.1 = (bf16[512,512]{1,0:T(8,128)(2,1)S(1)}, bf16[512,512]{1,0:T(8,128)(2,1)S(1)}, u32[]{:S(2)}, u32[]{:S(2)}) collective-permute-start(bf16[512,512]{1,0:T(8,128)(2,1)S(1)} %bitcast.9), channel_id=1, source_target_pairs={{0,2},{1,7},{2,4},{3,1},{4,6},{5,3},{6,0},{7,5},{8,10},{9,15},{10,... | collective-permute-start | bytes 1572872 | tf_op jit(solution)/shard_map/ppermute | solution.py:166
  38.6 0.0 collective-permute-done.theirs_ref
  38.6 6.1 %collective-permute-done.1.other_ref = bf16[512,512]{1,0:T(8,128)(2,1)S(1)} collective-permute-done((bf16[512,512]{1,0:T(8,128)(2,1)S(1)}, bf16[512,512]{1,0:T(8,128)(2,1)S(1)}, u32[]{:S(2)}, u32[]{:S(2)}) %collective-permute-start.1) | collective-permute-done | bytes 524320 | tf_op jit(solution)/shard_map/ppermute | solution.py:166
  44.7 2.1 %ladder.1 = f32[64,8,256]{2,1,0:T(8,128)} custom-call(bf16[2,256,1024]{2,1,0:T(8,128)(2,1)S(1)} %fusion.mine_ref, bf16[2,256,1024]{2,1,0:T(8,128)(2,1)S(1)} %collective-permute-done.theirs_ref, bf16[512,512]{1,0:T(8,128)(2,1)S(1)} %bitcast.10, bf16[512,512]{1,0:T(8,128)(2,1)S(1)} %collective-permute-done.1.other_ref), custom_call_target="tpu_custom_call" | custom-call | tf_op jit(solution)/shard_map/ladder/pallas_call | solution.py:112
  46.8 12.6 %all-to-all-start.1 = ((f32[64,8,256]{2,1,0:T(8,128)}), f32[64,8,256]{2,1,0:T(8,128)S(1)}, u32[]{:S(2)}, u32[]{:S(2)}) async-start(f32[64,8,256]{2,1,0:T(8,128)} %ladder.1), calls=%async_computation.1 | async-start | bytes 1048576 | tf_op jit(solution)/shard_map/all_to_all | solution.py:169
  59.4 0.8 %fusion.10 = (f32[32]{0:T(128)S(1)}, f32[32]{0:T(128)S(1)}) fusion(f32[768]{0:T(1024)} %param.15, s32[]{:T(128)S(6)} %select_n.94, s32[]{:T(128)S(6)} %select_n.95), kind=kLoop, calls=%fused_computation.27 | loop fusion | bytes 520 | tf_op jit(solution)/shard_map/dynamic_slice | solution.py:180
  60.2 0.0 copy-done.4
  60.2 0.1 broadcast_add_fusion
  60.3 9.4 %all-to-all-done.1 = f32[64,8,256]{2,1,0:T(8,128)S(1)} async-done(((f32[64,8,256]{2,1,0:T(8,128)}), f32[64,8,256]{2,1,0:T(8,128)S(1)}, u32[]{:S(2)}, u32[]{:S(2)}) %all-to-all-start.1) | async-done | bytes 524320 | tf_op jit(solution)/shard_map/all_to_all | solution.py:169
  69.7 0.1 reduce_sum.77
  69.8 4.7 %collective-permute-start.2 = (f32[4,256]{1,0:T(4,128)S(1)}, f32[4,256]{1,0:T(4,128)S(1)}, u32[]{:S(2)}, u32[]{:S(2)}) collective-permute-start(f32[4,256]{1,0:T(4,128)S(1)} %get-tuple-element.18), channel_id=1, source_target_pairs={{0,1},{1,0},{2,3},{3,2},{4,5},{5,4},{6,7},{7,6},{8,9},{9,8},{10,11... | collective-permute-start | bytes 12296 | tf_op jit(solution)/shard_map/ppermute | solution.py:172
  74.5 0.0 copy-done.2
  74.5 0.2 select_reduce_fusion
  74.7 0.1 add.49
  74.8 0.5 collective-permute-done.2
  75.3 0.7 fusion.1
  (5 shorter events, 0.0 us)
Async XLA Ops:
  0.0 22.6 %copy-start.3 = (s32[128]{0:T(128)S(1)}, s32[128]{0:T(128)}, u32[]{:S(2)}) copy-start(s32[128]{0:T(128)} %param.12) | copy-start | bytes 1540
  0.0 25.2 %copy-start = (bf16[256,2,1024]{2,1,0:T(2,128)(2,1)S(1)}, bf16[256,2,1024]{2,1,0:T(2,128)(2,1)}, u32[]{:S(2)}) copy-start(bf16[256,2,1024]{2,1,0:T(2,128)(2,1)} %param.9) | copy-start | bytes 3145732
  0.0 22.7 %copy-start.5 = (s32[128]{0:T(128)S(1)}, s32[128]{0:T(128)}, u32[]{:S(2)}) copy-start(s32[128]{0:T(128)} %param.11) | copy-start | bytes 1540
  0.0 22.9 %copy-start.1 = (s32[24]{0:T(128)S(1)}, s32[24]{0:T(128)}, u32[]{:S(2)}) copy-start(s32[24]{0:T(128)} %param.10) | copy-start | bytes 292
  2.5 31.6 %all-to-all-start = ((bf16[64,8,512]{2,1,0:T(8,128)(2,1)}), bf16[64,8,512]{2,1,0:T(8,128)(2,1)S(1)}, u32[]{:S(2)}, u32[]{:S(2)}) async-start(bf16[64,8,512]{2,1,0:T(8,128)(2,1)} %pack.1), calls=%async_computation | async-start | bytes 1048576 | tf_op jit(solution)/shard_map/all_to_all | solution.py:145
  25.6 13.0 %collective-permute-start = (bf16[2,256,1024]{2,1,0:T(8,128)(2,1)S(1)}, bf16[2,256,1024]{2,1,0:T(8,128)(2,1)S(1)}, u32[]{:S(2)}, u32[]{:S(2)}) collective-permute-start(bf16[2,256,1024]{2,1,0:T(8,128)(2,1)S(1)} %fusion.mine_ref), channel_id=1, source_target_pairs={{0,1},{1,0},{2,3},{3,2},{4,5},{5,4},{6,7},{7,6},{8,9},{9,8},{10,11... | collective-permute-start | bytes 3145736 | tf_op jit(solution)/shard_map/ppermute | solution.py:163
  34.1 26.1 %copy-start.4 = (s32[8,2]{0,1:T(2,128)S(1)}, s32[8,2]{0,1:T(2,128)}, u32[]{:S(2)}) copy-start(s32[8,2]{0,1:T(2,128)} %param.13) | copy-start | bytes 196
  34.1 40.4 %copy-start.2 = (f32[300]{0:T(512)S(1)}, f32[300]{0:T(512)}, u32[]{:S(2)}) copy-start(f32[300]{0:T(512)} %param.14) | copy-start | bytes 3604
  34.1 10.6 %collective-permute-start.1 = (bf16[512,512]{1,0:T(8,128)(2,1)S(1)}, bf16[512,512]{1,0:T(8,128)(2,1)S(1)}, u32[]{:S(2)}, u32[]{:S(2)}) collective-permute-start(bf16[512,512]{1,0:T(8,128)(2,1)S(1)} %bitcast.9), channel_id=1, source_target_pairs={{0,2},{1,7},{2,4},{3,1},{4,6},{5,3},{6,0},{7,5},{8,10},{9,15},{10,... | collective-permute-start | bytes 1572872 | tf_op jit(solution)/shard_map/ppermute | solution.py:166
  46.8 22.9 %all-to-all-start.1 = ((f32[64,8,256]{2,1,0:T(8,128)}), f32[64,8,256]{2,1,0:T(8,128)S(1)}, u32[]{:S(2)}, u32[]{:S(2)}) async-start(f32[64,8,256]{2,1,0:T(8,128)} %ladder.1), calls=%async_computation.1 | async-start | bytes 1048576 | tf_op jit(solution)/shard_map/all_to_all | solution.py:169
  69.8 5.5 %collective-permute-start.2 = (f32[4,256]{1,0:T(4,128)S(1)}, f32[4,256]{1,0:T(4,128)S(1)}, u32[]{:S(2)}, u32[]{:S(2)}) collective-permute-start(f32[4,256]{1,0:T(4,128)S(1)} %get-tuple-element.18), channel_id=1, source_target_pairs={{0,1},{1,0},{2,3},{3,2},{4,5},{5,4},{6,7},{7,6},{8,9},{9,8},{10,11... | collective-permute-start | bytes 12296 | tf_op jit(solution)/shard_map/ppermute | solution.py:172

commit v5 on v4

--- a/solution.py
+++ b/solution.py
@@ -23,10 +23,11 @@
     return (place + owners // 2 + owners // 16) % owners
 
 
-def pack_kernel(slot_ref, amp_ref, out_ref, slots_in, amp_in, rows, slot_sem, amp_sem):
-    owners, _, width = rows.shape
-    half, tiles, _ = amp_in.shape
+def pack_kernel(slot_ref, amp_ref, out_ref, slots_in, amp_in, slot_sem, amp_sem):
+    half, tiles, width = amp_in.shape
     slots = slots_in.shape[1]
+    owners, per_owner, _ = out_ref.shape
+    rows = owners * per_owner
     place = lax.axis_index("intg")
     share, core = place // CORES % SHARES, place % CORES
     slot_copy = pltpu.make_async_copy(slot_ref, slots_in, slot_sem)
@@ -39,26 +40,26 @@
     )
     slot_copy.start()
     amp_copy.start()
+    row_at = lax.broadcasted_iota(jnp.int32, (rows, slots), 0)
+    slot_at = lax.broadcasted_iota(jnp.int32, (rows, slots), 1)
+    owner_at = owner_in_turn(owners, row_at // per_owner)
+    wanted = owner_at * SLOTS + row_at // half % SLOTS
+    mine = jnp.where(slot_at == wanted, 1.0, 0.0).astype(jnp.bfloat16)
+    j_at = lax.broadcasted_iota(jnp.int32, (rows, tiles), 0) % half
     tile_at = lax.broadcasted_iota(jnp.int32, (tiles, slots), 0)
-    owner_at = owner_in_turn(owners, lax.broadcasted_iota(jnp.int32, (owners, slots), 0))
-    slot_at = lax.broadcasted_iota(jnp.int32, (owners, slots), 1)
     slot_copy.wait()
     held = jnp.where(tile_at == slots_in[...], 1.0, 0.0).astype(jnp.bfloat16)
-    select = []
-    for slot in range(SLOTS):
-        mine = jnp.where(slot_at == owner_at * SLOTS + slot, 1.0, 0.0).astype(jnp.bfloat16)
-        select.append(
-            lax.dot_general(
-                mine, held, (((1,), (1,)), ((), ())), preferred_element_type=jnp.float32
-            ).astype(jnp.bfloat16)
-        )
-    select = jnp.concatenate(select)
+    tile_of = lax.dot_general(
+        mine, held, (((1,), (1,)), ((), ())), preferred_element_type=jnp.float32
+    )
+    select = jnp.concatenate(
+        [jnp.where(j_at == j, tile_of, 0.0).astype(jnp.bfloat16) for j in range(half)], axis=1
+    )
     amp_copy.wait()
-    for j in range(half):
-        picked = jnp.dot(select, amp_in[j], preferred_element_type=jnp.float32)
-        for slot in range(SLOTS):
-            rows[:, slot * half + j, :] = picked[slot * owners : (slot + 1) * owners]
-    out_ref[...] = rows[...].astype(jnp.bfloat16)
+    picked = jnp.dot(
+        select, amp_in[...].reshape(half * tiles, width), preferred_element_type=jnp.float32
+    )
+    out_ref[...] = picked.astype(jnp.bfloat16).reshape(out_ref.shape)
 
 
 def pack(slot_tiles, amplitudes, owners, width):
@@ -72,7 +73,6 @@
         scratch_shapes=[
             pltpu.VMEM((1, slot_tiles.shape[0]), jnp.int32),
             pltpu.VMEM((half, tiles, width), jnp.bfloat16),
-            pltpu.VMEM((owners, SLOTS * half, width), jnp.float32),
             pltpu.SemaphoreType.DMA,
             pltpu.SemaphoreType.DMA,
         ],
@@ -84,39 +84,39 @@
     )
 
 
-def ladder_kernel(half, mine_ref, theirs_ref, piece_ref, other_ref, out_ref):
-    width = piece_ref.shape[1]
-    share = lax.axis_index("intg") // CORES % SHARES
-    here = pl.ds(pl.multiple_of(share * width, width), width)
-    there = pl.ds(pl.multiple_of((1 - share) * width, width), width)
-
-    def dot(rows, ints):
+def ladder_kernel(half, away, mine_ref, theirs_ref, columns_ref, *refs):
+    out_ref = refs[-1]
+    width = columns_ref.shape[1]
+    share = (lax.axis_index("intg") // CORES + away) % SHARES
+    entries = pl.ds(pl.multiple_of(share * width, width), width)
+
+    def product(ints_ref, slot):
         return lax.dot_general(
-            rows, ints, (((1,), (1,)), ((), ())), preferred_element_type=jnp.float32
-        )
-
-    def product(ints_ref, slot):
-        total = dot(piece_ref[...], ints_ref[slot, :, here]) + dot(
-            other_ref[...], ints_ref[slot, :, there]
-        )
-        return total.reshape(out_ref.shape)
+            columns_ref[...],
+            ints_ref[slot, :, entries],
+            (((1,), (1,)), ((), ())),
+            preferred_element_type=jnp.float32,
+        ).reshape(out_ref.shape)
 
     first = lax.broadcasted_iota(jnp.int32, out_ref.shape, 1) < half
     kept = jnp.where(first, product(mine_ref, 0), product(theirs_ref, 1))
     moved = jnp.where(first, product(theirs_ref, 0), product(mine_ref, 1))
-    out_ref[...] = kept + pltpu.roll(moved, half, 1)
-
-
-def ladder_sums(owners, half, mine, theirs, piece, other):
-    cols = mine.shape[1]
+    total = kept + pltpu.roll(moved, half, 1)
+    for sum_ref in refs[:-1]:
+        total = total + sum_ref[...]
+    out_ref[...] = total
+
+
+def ladder_sums(owners, half, away, *operands):
+    cols = operands[0].shape[1]
     return pl.pallas_call(
-        functools.partial(ladder_kernel, half),
+        functools.partial(ladder_kernel, half, away),
         out_shape=jax.ShapeDtypeStruct((owners, CORES * half, cols), jnp.float32),
-        in_specs=[pl.BlockSpec(memory_space=pltpu.VMEM)] * 4,
+        in_specs=[pl.BlockSpec(memory_space=pltpu.VMEM)] * len(operands),
         out_specs=pl.BlockSpec(memory_space=pltpu.VMEM),
         compiler_params=pltpu.CompilerParams(vmem_limit_bytes=24 << 20),
         name="ladder",
-    )(mine, theirs, piece, other)
+    )(*operands)
 
 
 def on_device(
@@ -165,7 +165,8 @@
     ring = [(i, (i + (CORES if i % CORES == 0 else -CORES)) % n_intg) for i in range(n_intg)]
     other = lax.ppermute(piece, "intg", ring)
     half = pairs // CORES
-    partial = ladder_sums(n_pair, half, masked_ints, other_ints, piece, other)
+    partial = ladder_sums(n_pair, half, 0, masked_ints, other_ints, piece)
+    partial = ladder_sums(n_pair, half, 1, masked_ints, other_ints, other, partial)
     parts = lax.all_to_all(partial, "pair", split_axis=0, concat_axis=0, tiled=True, axis_index_groups=in_turn)
     halves = jnp.sum(parts, axis=0)
     kept = halves[:half]

time: 76.4 us -> 75.7 us (level)
  waiting for transfers between devices: 21.4 us -> 20.6 us
    ppermute x1, waiting for transfers between devices: 6.09 us -> 5.3 us  [on_device(): other = lax.ppermute(piece, 'intg', ring)]
    pallas_call x1 -> x2, Pallas kernels: 2.07 us -> 2.3 us  [ladder_sums(): pl.pallas_call(functools.partial(ladder_kernel, half, away), out_shape=ja...]
  transfers between devices with their start and end apart: 5 -> 5, of which waited for: 4 -> 4; matrix products, arithmetic and copies ran while one was open for 4% -> 4% of each run, Pallas kernels for 0% -> 1%
where the time goes in v5:
time: 75.7 us; the launch traced here: 75.2 us
  starting transfers between devices  44.9 us (59%)
  waiting for transfers between devices  20.6 us (27%)
  Pallas kernels  4.69 us (6%)
  other arithmetic  2.61 us (3%)
  between operations  1.57 us (2%)
  local copies, waits for them, and re-layouts  0.96 us (1%)
    all_to_all x1, starting transfers between devices, on_device(): lax.all_to_all(send, 'pair', split_axis=0, concat_axis=0, tiled=True, axi...  20.1 us
    all_to_all x1, starting transfers between devices, on_device(): lax.all_to_all(partial, 'pair', split_axis=0, concat_axis=0, tiled=True,...  12.6 us
    all_to_all x1, waiting for transfers between devices, on_device(): lax.all_to_all(partial, 'pair', split_axis=0, concat_axis=0, tiled=True,...  9.39 us
    all_to_all x1, waiting for transfers between devices, on_device(): lax.all_to_all(send, 'pair', split_axis=0, concat_axis=0, tiled=True, axi...  5.37 us
    ppermute x1, waiting for transfers between devices, on_device(): other = lax.ppermute(piece, 'intg', ring)  5.3 us
    ppermute x1, starting transfers between devices, on_device(): came = lax.ppermute(halves[half:], 'intg', swap)  4.68 us
    ppermute x1, starting transfers between devices, on_device(): other = lax.ppermute(piece, 'intg', ring)  4.38 us
    ppermute x1, starting transfers between devices, on_device(): other_ints = lax.ppermute(masked_ints, 'intg', swap)  3.14 us
  transfers between devices with their start and end apart: 5, of which 4 were waited for; matrix products, arithmetic and copies ran while one was open for 4% of the time, Pallas kernels for 1%

profile of v5, /device:TPU:1, one launch (start us, length us, event | category | flops | bytes accessed | tf_op | source)
XLA Modules:
  0.0 75.2 jit_solution(2530360062981526831)
XLA Ops:
  0.0 0.0 copy-start.3
  0.0 0.0 copy-start
  0.0 0.0 copy-start.5
  0.0 0.0 copy-start.1
  0.0 2.4 %pack.1 = bf16[64,8,512]{2,1,0:T(8,128)(2,1)} custom-call(s32[1,128]{1,0:T(1,128)} %bitcast.12, bf16[8,128,1024]{2,1,0:T(8,128)(2,1)} %amp_ref.1), custom_call_target="tpu_custom_call" | custom-call | tf_op jit(solution)/shard_map/pack/pallas_call | solution.py:68
  2.4 20.1 %all-to-all-start = ((bf16[64,8,512]{2,1,0:T(8,128)(2,1)}), bf16[64,8,512]{2,1,0:T(8,128)(2,1)S(1)}, u32[]{:S(2)}, u32[]{:S(2)}) async-start(bf16[64,8,512]{2,1,0:T(8,128)(2,1)} %pack.1), calls=%async_computation | async-start | bytes 1048576 | tf_op jit(solution)/shard_map/all_to_all | solution.py:145
  22.5 0.0 copy-done.3
  22.5 0.1 and_select_fusion.1
  22.6 0.0 copy-done.5
  22.7 0.2 fusion.4
  22.9 0.0 copy-done.1
  22.9 0.2 fusion.3
  23.1 0.7 fusion.6
  25.2 0.0 copy-done
  25.2 0.3 fusion.mine_ref
  25.5 3.1 %collective-permute-start = (bf16[2,256,1024]{2,1,0:T(8,128)(2,1)S(1)}, bf16[2,256,1024]{2,1,0:T(8,128)(2,1)S(1)}, u32[]{:S(2)}, u32[]{:S(2)}) collective-permute-start(bf16[2,256,1024]{2,1,0:T(8,128)(2,1)S(1)} %fusion.mine_ref), channel_id=1, source_target_pairs={{0,1},{1,0},{2,3},{3,2},{4,5},{5,4},{6,7},{7,6},{8,9},{9,8},{10,11... | collective-permute-start | bytes 3145736 | tf_op jit(solution)/shard_map/ppermute | solution.py:163
  28.7 5.4 %all-to-all-done = bf16[64,8,512]{2,1,0:T(8,128)(2,1)S(1)} async-done(((bf16[64,8,512]{2,1,0:T(8,128)(2,1)}), bf16[64,8,512]{2,1,0:T(8,128)(2,1)S(1)}, u32[]{:S(2)}, u32[]{:S(2)}) %all-to-all-start) | async-done | bytes 524320 | tf_op jit(solution)/shard_map/all_to_all | solution.py:145
  34.0 4.4 %collective-permute-start.1 = (bf16[512,512]{1,0:T(8,128)(2,1)S(1)}, bf16[512,512]{1,0:T(8,128)(2,1)S(1)}, u32[]{:S(2)}, u32[]{:S(2)}) collective-permute-start(bf16[512,512]{1,0:T(8,128)(2,1)S(1)} %bitcast.9), channel_id=1, source_target_pairs={{0,2},{1,7},{2,4},{3,1},{4,6},{5,3},{6,0},{7,5},{8,10},{9,15},{10,... | collective-permute-start | bytes 1572872 | tf_op jit(solution)/shard_map/ppermute | solution.py:166
  38.4 0.0 collective-permute-done.theirs_ref
  38.4 0.8 %ladder.2.refs_0_ = f32[64,8,256]{2,1,0:T(8,128)S(1)} custom-call(bf16[2,256,1024]{2,1,0:T(8,128)(2,1)S(1)} %fusion.mine_ref, bf16[2,256,1024]{2,1,0:T(8,128)(2,1)S(1)} %collective-permute-done.theirs_ref, bf16[512,512]{1,0:T(8,128)(2,1)S(1)} %bitcast.10), custom_call_target="tpu_custom_call" | custom-call | tf_op jit(solution)/shard_map/ladder/pallas_call | solution.py:112
  39.2 0.0 copy-start.4
  39.2 0.0 copy-start.2
  39.2 5.3 %collective-permute-done.1.columns_ref = bf16[512,512]{1,0:T(8,128)(2,1)S(1)} collective-permute-done((bf16[512,512]{1,0:T(8,128)(2,1)S(1)}, bf16[512,512]{1,0:T(8,128)(2,1)S(1)}, u32[]{:S(2)}, u32[]{:S(2)}) %collective-permute-start.1) | collective-permute-done | bytes 524320 | tf_op jit(solution)/shard_map/ppermute | solution.py:166
  44.5 1.5 %ladder.3 = f32[64,8,256]{2,1,0:T(8,128)} custom-call(bf16[2,256,1024]{2,1,0:T(8,128)(2,1)S(1)} %fusion.mine_ref, bf16[2,256,1024]{2,1,0:T(8,128)(2,1)S(1)} %collective-permute-done.theirs_ref, bf16[512,512]{1,0:T(8,128)(2,1)S(1)} %collective-permute-done.1.columns_ref, f32[64,8,256]{2,1,0:T(8,128)S(1)} %ladder.2.refs_0_), custom_call_target="tpu_custom_call" | custom-call | tf_op jit(solution)/shard_map/ladder/pallas_call | solution.py:112
  46.1 12.6 %all-to-all-start.1 = ((f32[64,8,256]{2,1,0:T(8,128)}), f32[64,8,256]{2,1,0:T(8,128)S(1)}, u32[]{:S(2)}, u32[]{:S(2)}) async-start(f32[64,8,256]{2,1,0:T(8,128)} %ladder.3), calls=%async_computation.1 | async-start | bytes 1048576 | tf_op jit(solution)/shard_map/all_to_all | solution.py:170
  58.7 0.8 %fusion.10 = (f32[32]{0:T(128)S(1)}, f32[32]{0:T(128)S(1)}) fusion(f32[768]{0:T(1024)} %param.15, s32[]{:T(128)S(6)} %select_n.94, s32[]{:T(128)S(6)} %select_n.95), kind=kLoop, calls=%fused_computation.27 | loop fusion | bytes 520 | tf_op jit(solution)/shard_map/dynamic_slice | solution.py:181
  59.5 0.0 copy-done.4
  59.5 0.1 broadcast_add_fusion
  59.6 9.4 %all-to-all-done.1 = f32[64,8,256]{2,1,0:T(8,128)S(1)} async-done(((f32[64,8,256]{2,1,0:T(8,128)}), f32[64,8,256]{2,1,0:T(8,128)S(1)}, u32[]{:S(2)}, u32[]{:S(2)}) %all-to-all-start.1) | async-done | bytes 524320 | tf_op jit(solution)/shard_map/all_to_all | solution.py:170
  69.0 0.1 reduce_sum.77
  69.1 4.7 %collective-permute-start.2 = (f32[4,256]{1,0:T(4,128)S(1)}, f32[4,256]{1,0:T(4,128)S(1)}, u32[]{:S(2)}, u32[]{:S(2)}) collective-permute-start(f32[4,256]{1,0:T(4,128)S(1)} %get-tuple-element.18), channel_id=1, source_target_pairs={{0,1},{1,0},{2,3},{3,2},{4,5},{5,4},{6,7},{7,6},{8,9},{9,8},{10,11... | collective-permute-start | bytes 12296 | tf_op jit(solution)/shard_map/ppermute | solution.py:173
  73.8 0.0 copy-done.2
  73.8 0.2 select_reduce_fusion
  74.0 0.1 add.49
  74.1 0.5 collective-permute-done.2
  74.6 0.7 fusion.1
  (5 shorter events, 0.0 us)
Async XLA Ops:
  0.0 22.5 %copy-start.3 = (s32[128]{0:T(128)S(1)}, s32[128]{0:T(128)}, u32[]{:S(2)}) copy-start(s32[128]{0:T(128)} %param.12) | copy-start | bytes 1540
  0.0 25.2 %copy-start = (bf16[256,2,1024]{2,1,0:T(2,128)(2,1)S(1)}, bf16[256,2,1024]{2,1,0:T(2,128)(2,1)}, u32[]{:S(2)}) copy-start(bf16[256,2,1024]{2,1,0:T(2,128)(2,1)} %param.9) | copy-start | bytes 3145732
  0.0 22.6 %copy-start.5 = (s32[128]{0:T(128)S(1)}, s32[128]{0:T(128)}, u32[]{:S(2)}) copy-start(s32[128]{0:T(128)} %param.11) | copy-start | bytes 1540
  0.0 22.8 %copy-start.1 = (s32[24]{0:T(128)S(1)}, s32[24]{0:T(128)}, u32[]{:S(2)}) copy-start(s32[24]{0:T(128)} %param.10) | copy-start | bytes 292
  2.4 31.6 %all-to-all-start = ((bf16[64,8,512]{2,1,0:T(8,128)(2,1)}), bf16[64,8,512]{2,1,0:T(8,128)(2,1)S(1)}, u32[]{:S(2)}, u32[]{:S(2)}) async-start(bf16[64,8,512]{2,1,0:T(8,128)(2,1)} %pack.1), calls=%async_computation | async-start | bytes 1048576 | tf_op jit(solution)/shard_map/all_to_all | solution.py:145
  25.5 12.9 %collective-permute-start = (bf16[2,256,1024]{2,1,0:T(8,128)(2,1)S(1)}, bf16[2,256,1024]{2,1,0:T(8,128)(2,1)S(1)}, u32[]{:S(2)}, u32[]{:S(2)}) collective-permute-start(bf16[2,256,1024]{2,1,0:T(8,128)(2,1)S(1)} %fusion.mine_ref), channel_id=1, source_target_pairs={{0,1},{1,0},{2,3},{3,2},{4,5},{5,4},{6,7},{7,6},{8,9},{9,8},{10,11... | collective-permute-start | bytes 3145736 | tf_op jit(solution)/shard_map/ppermute | solution.py:163
  34.0 10.5 %collective-permute-start.1 = (bf16[512,512]{1,0:T(8,128)(2,1)S(1)}, bf16[512,512]{1,0:T(8,128)(2,1)S(1)}, u32[]{:S(2)}, u32[]{:S(2)}) collective-permute-start(bf16[512,512]{1,0:T(8,128)(2,1)S(1)} %bitcast.9), channel_id=1, source_target_pairs={{0,2},{1,7},{2,4},{3,1},{4,6},{5,3},{6,0},{7,5},{8,10},{9,15},{10,... | collective-permute-start | bytes 1572872 | tf_op jit(solution)/shard_map/ppermute | solution.py:166
  39.2 20.3 %copy-start.4 = (s32[8,2]{0,1:T(2,128)S(1)}, s32[8,2]{0,1:T(2,128)}, u32[]{:S(2)}) copy-start(s32[8,2]{0,1:T(2,128)} %param.13) | copy-start | bytes 196
  39.2 34.5 %copy-start.2 = (f32[300]{0:T(512)S(1)}, f32[300]{0:T(512)}, u32[]{:S(2)}) copy-start(f32[300]{0:T(512)} %param.14) | copy-start | bytes 3604
  46.1 22.9 %all-to-all-start.1 = ((f32[64,8,256]{2,1,0:T(8,128)}), f32[64,8,256]{2,1,0:T(8,128)S(1)}, u32[]{:S(2)}, u32[]{:S(2)}) async-start(f32[64,8,256]{2,1,0:T(8,128)} %ladder.3), calls=%async_computation.1 | async-start | bytes 1048576 | tf_op jit(solution)/shard_map/all_to_all | solution.py:170
  69.1 5.5 %collective-permute-start.2 = (f32[4,256]{1,0:T(4,128)S(1)}, f32[4,256]{1,0:T(4,128)S(1)}, u32[]{:S(2)}, u32[]{:S(2)}) collective-permute-start(f32[4,256]{1,0:T(4,128)S(1)} %get-tuple-element.18), channel_id=1, source_target_pairs={{0,1},{1,0},{2,3},{3,2},{4,5},{5,4},{6,7},{7,6},{8,9},{9,8},{10,11... | collective-permute-start | bytes 12296 | tf_op jit(solution)/shard_map/ppermute | solution.py:173

commit v6 on v5

--- a/solution.py
+++ b/solution.py
@@ -165,6 +165,17 @@
     ring = [(i, (i + (CORES if i % CORES == 0 else -CORES)) % n_intg) for i in range(n_intg)]
     other = lax.ppermute(piece, "intg", ring)
     half = pairs // CORES
+    occupied_sum = lookup(occupied_energy, pair_list[:, 0]) + lookup(
+        occupied_energy, pair_list[:, 1]
+    )
+    first_energy = lax.dynamic_slice_in_dim(virtual_energy, first_tile * TILE, TILE)
+    second_energy = lax.dynamic_slice_in_dim(virtual_energy, second_tile * TILE, TILE)
+    virtual_sum = jnp.repeat(first_energy[: ab_rows // TILE], TILE) + jnp.tile(
+        second_energy, ab_rows // TILE
+    )
+    denom = occupied_sum[:, None] - virtual_sum[None, :]
+    other, denom = lax.optimization_barrier((other, denom))
+
     partial = ladder_sums(n_pair, half, 0, masked_ints, other_ints, piece)
     partial = ladder_sums(n_pair, half, 1, masked_ints, other_ints, other, partial)
     parts = lax.all_to_all(partial, "pair", split_axis=0, concat_axis=0, tiled=True, axis_index_groups=in_turn)
@@ -175,15 +186,6 @@
         block % CORES == 0, jnp.concatenate([kept, came]), jnp.concatenate([came, kept])
     )
 
-    occupied_sum = lookup(occupied_energy, pair_list[:, 0]) + lookup(
-        occupied_energy, pair_list[:, 1]
-    )
-    first_energy = lax.dynamic_slice_in_dim(virtual_energy, first_tile * TILE, TILE)
-    second_energy = lax.dynamic_slice_in_dim(virtual_energy, second_tile * TILE, TILE)
-    virtual_sum = jnp.repeat(first_energy[: ab_rows // TILE], TILE) + jnp.tile(
-        second_energy, ab_rows // TILE
-    )
-    denom = occupied_sum[:, None] - virtual_sum[None, :]
     return ladder / denom
 
 

time: 75.7 us -> 74.5 us (0.984)
  blocking collectives: 0 us -> 22.7 us
  starting transfers between devices: 44.9 us -> 32.3 us
  waiting for transfers between devices: 20.6 us -> 10.2 us
  Pallas kernels: 4.69 us -> 3.89 us
    all_to_all x0 -> x1, blocking collectives: none -> 22.7 us  [on_device(): lax.all_to_all(partial, 'pair', split_axis=0, concat_axis=0, tiled=True,...]
    all_to_all x1 -> x0, starting transfers between devices: 12.6 us -> none  [on_device(): lax.all_to_all(partial, 'pair', split_axis=0, concat_axis=0, tiled=True,...]
    all_to_all x1 -> x0, waiting for transfers between devices: 9.39 us -> none  [on_device(): lax.all_to_all(partial, 'pair', split_axis=0, concat_axis=0, tiled=True,...]
    all_to_all x1, waiting for transfers between devices: 5.37 us -> 4.36 us  [on_device(): lax.all_to_all(send, 'pair', split_axis=0, concat_axis=0, tiled=True, axi...]
    pallas_call x2, Pallas kernels: 2.3 us -> 1.49 us  [ladder_sums(): pl.pallas_call(functools.partial(ladder_kernel, half, away), out_shape=ja...]
  transfers between devices with their start and end apart: 5 -> 4, of which waited for: 4 -> 3; matrix products, arithmetic and copies ran while one was open for 4% -> 4% of each run, Pallas kernels for 1% -> 1%
where the time goes in v6:
time: 74.5 us; the launch traced here: 74.2 us
  starting transfers between devices  32.3 us (43%)
  blocking collectives  22.7 us (30%)
  waiting for transfers between devices  10.2 us (14%)
  Pallas kernels  3.89 us (5%)
  other arithmetic  2.62 us (4%)
  between operations  1.58 us (2%)
  local copies, waits for them, and re-layouts  0.96 us (1%)
    all_to_all x1, blocking collectives, on_device(): lax.all_to_all(partial, 'pair', split_axis=0, concat_axis=0, tiled=True,...  22.7 us
    all_to_all x1, starting transfers between devices, on_device(): lax.all_to_all(send, 'pair', split_axis=0, concat_axis=0, tiled=True, axi...  20.1 us
    ppermute x1, waiting for transfers between devices, on_device(): other = lax.ppermute(piece, 'intg', ring)  5.01 us
    ppermute x1, starting transfers between devices, on_device(): came = lax.ppermute(halves[half:], 'intg', swap)  4.66 us
    ppermute x1, starting transfers between devices, on_device(): other = lax.ppermute(piece, 'intg', ring)  4.38 us
    all_to_all x1, waiting for transfers between devices, on_device(): lax.all_to_all(send, 'pair', split_axis=0, concat_axis=0, tiled=True, axi...  4.36 us
    ppermute x1, starting transfers between devices, on_device(): other_ints = lax.ppermute(masked_ints, 'intg', swap)  3.14 us
    pallas_call x1, Pallas kernels, pack(): pl.pallas_call(pack_kernel, out_shape=jax.ShapeDtypeStruct((owners, SLOTS...  2.39 us
  transfers between devices with their start and end apart: 4, of which 3 were waited for; matrix products, arithmetic and copies ran while one was open for 4% of the time, Pallas kernels for 1%

profile of v6, /device:TPU:1, one launch (start us, length us, event | category | flops | bytes accessed | tf_op | source)
XLA Modules:
  0.0 74.2 jit_solution(14704222244859474714)
XLA Ops:
  0.0 0.0 copy-start.3
  0.0 0.0 copy-start
  0.0 0.0 copy-start.5
  0.0 0.0 copy-start.1
  0.0 2.4 %pack.1 = bf16[64,8,512]{2,1,0:T(8,128)(2,1)} custom-call(s32[1,128]{1,0:T(1,128)} %bitcast.12, bf16[8,128,1024]{2,1,0:T(8,128)(2,1)} %amp_ref.1), custom_call_target="tpu_custom_call" | custom-call | tf_op jit(solution)/shard_map/pack/pallas_call | solution.py:68
  2.4 0.0 copy-start.4
  2.4 0.0 copy-start.2
  2.4 20.1 %all-to-all-start = ((bf16[64,8,512]{2,1,0:T(8,128)(2,1)}), bf16[64,8,512]{2,1,0:T(8,128)(2,1)S(1)}, u32[]{:S(2)}, u32[]{:S(2)}) async-start(bf16[64,8,512]{2,1,0:T(8,128)(2,1)} %pack.1), calls=%async_computation | async-start | bytes 1048576 | tf_op jit(solution)/shard_map/all_to_all | solution.py:145
  22.6 0.0 copy-done.3
  22.6 0.1 and_select_fusion.1
  22.7 0.0 copy-done.5
  22.7 0.2 fusion.4
  22.9 0.0 copy-done.1
  22.9 0.2 fusion.3
  23.1 0.7 fusion.6
  25.2 0.0 copy-done
  25.2 0.3 fusion.mine_ref
  25.5 3.1 %collective-permute-start = (bf16[2,256,1024]{2,1,0:T(8,128)(2,1)S(1)}, bf16[2,256,1024]{2,1,0:T(8,128)(2,1)S(1)}, u32[]{:S(2)}, u32[]{:S(2)}) collective-permute-start(bf16[2,256,1024]{2,1,0:T(8,128)(2,1)S(1)} %fusion.mine_ref), channel_id=1, source_target_pairs={{0,1},{1,0},{2,3},{3,2},{4,5},{5,4},{6,7},{7,6},{8,9},{9,8},{10,11... | collective-permute-start | bytes 3145736 | tf_op jit(solution)/shard_map/ppermute | solution.py:163
  28.7 0.8 %fusion.10 = (f32[32]{0:T(128)S(1)}, f32[32]{0:T(128)S(1)}) fusion(f32[768]{0:T(1024)} %param.15, s32[]{:T(128)S(6)} %select_n.93, s32[]{:T(128)S(6)} %select_n.94), kind=kLoop, calls=%fused_computation.28 | loop fusion | bytes 520 | tf_op jit(solution)/shard_map/dynamic_slice | solution.py:171
  29.6 0.1 broadcast_add_fusion
  29.6 0.1 add.49
  29.7 4.4 %all-to-all-done = bf16[64,8,512]{2,1,0:T(8,128)(2,1)S(1)} async-done(((bf16[64,8,512]{2,1,0:T(8,128)(2,1)}), bf16[64,8,512]{2,1,0:T(8,128)(2,1)S(1)}, u32[]{:S(2)}, u32[]{:S(2)}) %all-to-all-start) | async-done | bytes 524320 | tf_op jit(solution)/shard_map/all_to_all | solution.py:145
  34.1 4.4 %collective-permute-start.1 = (bf16[512,512]{1,0:T(8,128)(2,1)S(1)}, bf16[512,512]{1,0:T(8,128)(2,1)S(1)}, u32[]{:S(2)}, u32[]{:S(2)}) collective-permute-start(bf16[512,512]{1,0:T(8,128)(2,1)S(1)} %bitcast.9), channel_id=1, source_target_pairs={{0,2},{1,7},{2,4},{3,1},{4,6},{5,3},{6,0},{7,5},{8,10},{9,15},{10,... | collective-permute-start | bytes 1572872 | tf_op jit(solution)/shard_map/ppermute | solution.py:166
  38.5 0.0 copy-done.4
  38.5 0.0 copy-done.2
  38.5 0.2 select_reduce_fusion
  38.7 0.1 broadcast_subtract_fusion
  38.8 0.0 collective-permute-done.theirs_ref
  38.8 0.8 %ladder.2.refs_0_ = f32[64,8,256]{2,1,0:T(8,128)S(1)} custom-call(bf16[2,256,1024]{2,1,0:T(8,128)(2,1)S(1)} %fusion.mine_ref, bf16[2,256,1024]{2,1,0:T(8,128)(2,1)S(1)} %collective-permute-done.theirs_ref, bf16[512,512]{1,0:T(8,128)(2,1)S(1)} %bitcast.10), custom_call_target="tpu_custom_call" | custom-call | tf_op jit(solution)/shard_map/ladder/pallas_call | solution.py:112
  39.5 5.0 %collective-permute-done.1.columns_ref = bf16[512,512]{1,0:T(8,128)(2,1)S(1)} collective-permute-done((bf16[512,512]{1,0:T(8,128)(2,1)S(1)}, bf16[512,512]{1,0:T(8,128)(2,1)S(1)}, u32[]{:S(2)}, u32[]{:S(2)}) %collective-permute-start.1) | collective-permute-done | bytes 524320 | tf_op jit(solution)/shard_map/ppermute | solution.py:166
  44.6 0.7 %ladder.3 = f32[64,8,256]{2,1,0:T(8,128)S(1)} custom-call(bf16[2,256,1024]{2,1,0:T(8,128)(2,1)S(1)} %fusion.mine_ref, bf16[2,256,1024]{2,1,0:T(8,128)(2,1)S(1)} %collective-permute-done.theirs_ref, bf16[512,512]{1,0:T(8,128)(2,1)S(1)} %collective-permute-done.1.columns_ref, f32[64,8,256]{2,1,0:T(8,128)S(1)} %ladder.2.refs_0_), custom_call_target="tpu_custom_call" | custom-call | tf_op jit(solution)/shard_map/ladder/pallas_call | solution.py:112
  45.3 22.7 %all_to_all.10 = f32[64,8,256]{2,1,0:T(8,128)S(1)} all-to-all(f32[64,8,256]{2,1,0:T(8,128)S(1)} %ladder.3), channel_id=1, replica_groups={{288,296,304,312,320,328,336,344,352,360,368,376,384,392,400,408,416,42..., dimensions={0} | all-to-all | bytes 1048576 | tf_op jit(solution)/shard_map/all_to_all | solution.py:181
  68.0 0.1 reduce_sum.79
  68.1 4.7 %collective-permute-start.2 = (f32[4,256]{1,0:T(4,128)S(1)}, f32[4,256]{1,0:T(4,128)S(1)}, u32[]{:S(2)}, u32[]{:S(2)}) collective-permute-start(f32[4,256]{1,0:T(4,128)S(1)} %get-tuple-element.22), channel_id=1, source_target_pairs={{0,1},{1,0},{2,3},{3,2},{4,5},{5,4},{6,7},{7,6},{8,9},{9,8},{10,11... | collective-permute-start | bytes 12296 | tf_op jit(solution)/shard_map/ppermute | solution.py:184
  72.8 0.8 %collective-permute-done.2 = f32[4,256]{1,0:T(4,128)S(1)} collective-permute-done((f32[4,256]{1,0:T(4,128)S(1)}, f32[4,256]{1,0:T(4,128)S(1)}, u32[]{:S(2)}, u32[]{:S(2)}) %collective-permute-start.2) | collective-permute-done | bytes 4128 | tf_op jit(solution)/shard_map/ppermute | solution.py:184
  73.6 0.6 fusion.1
  (5 shorter events, 0.0 us)
Async XLA Ops:
  0.0 22.6 %copy-start.3 = (s32[128]{0:T(128)S(1)}, s32[128]{0:T(128)}, u32[]{:S(2)}) copy-start(s32[128]{0:T(128)} %param.12) | copy-start | bytes 1540
  0.0 25.2 %copy-start = (bf16[256,2,1024]{2,1,0:T(2,128)(2,1)S(1)}, bf16[256,2,1024]{2,1,0:T(2,128)(2,1)}, u32[]{:S(2)}) copy-start(bf16[256,2,1024]{2,1,0:T(2,128)(2,1)} %param.9) | copy-start | bytes 3145732
  0.0 22.7 %copy-start.5 = (s32[128]{0:T(128)S(1)}, s32[128]{0:T(128)}, u32[]{:S(2)}) copy-start(s32[128]{0:T(128)} %param.11) | copy-start | bytes 1540
  0.0 22.9 %copy-start.1 = (s32[24]{0:T(128)S(1)}, s32[24]{0:T(128)}, u32[]{:S(2)}) copy-start(s32[24]{0:T(128)} %param.10) | copy-start | bytes 292
  2.4 36.0 %copy-start.4 = (s32[8,2]{0,1:T(2,128)S(1)}, s32[8,2]{0,1:T(2,128)}, u32[]{:S(2)}) copy-start(s32[8,2]{0,1:T(2,128)} %param.13) | copy-start | bytes 196
  2.4 36.0 %copy-start.2 = (f32[300]{0:T(512)S(1)}, f32[300]{0:T(512)}, u32[]{:S(2)}) copy-start(f32[300]{0:T(512)} %param.14) | copy-start | bytes 3604
  2.4 31.6 %all-to-all-start = ((bf16[64,8,512]{2,1,0:T(8,128)(2,1)}), bf16[64,8,512]{2,1,0:T(8,128)(2,1)S(1)}, u32[]{:S(2)}, u32[]{:S(2)}) async-start(bf16[64,8,512]{2,1,0:T(8,128)(2,1)} %pack.1), calls=%async_computation | async-start | bytes 1048576 | tf_op jit(solution)/shard_map/all_to_all | solution.py:145
  25.5 13.2 %collective-permute-start = (bf16[2,256,1024]{2,1,0:T(8,128)(2,1)S(1)}, bf16[2,256,1024]{2,1,0:T(8,128)(2,1)S(1)}, u32[]{:S(2)}, u32[]{:S(2)}) collective-permute-start(bf16[2,256,1024]{2,1,0:T(8,128)(2,1)S(1)} %fusion.mine_ref), channel_id=1, source_target_pairs={{0,1},{1,0},{2,3},{3,2},{4,5},{5,4},{6,7},{7,6},{8,9},{9,8},{10,11... | collective-permute-start | bytes 3145736 | tf_op jit(solution)/shard_map/ppermute | solution.py:163
  34.1 10.5 %collective-permute-start.1 = (bf16[512,512]{1,0:T(8,128)(2,1)S(1)}, bf16[512,512]{1,0:T(8,128)(2,1)S(1)}, u32[]{:S(2)}, u32[]{:S(2)}) collective-permute-start(bf16[512,512]{1,0:T(8,128)(2,1)S(1)} %bitcast.9), channel_id=1, source_target_pairs={{0,2},{1,7},{2,4},{3,1},{4,6},{5,3},{6,0},{7,5},{8,10},{9,15},{10,... | collective-permute-start | bytes 1572872 | tf_op jit(solution)/shard_map/ppermute | solution.py:166
  68.1 5.5 %collective-permute-start.2 = (f32[4,256]{1,0:T(4,128)S(1)}, f32[4,256]{1,0:T(4,128)S(1)}, u32[]{:S(2)}, u32[]{:S(2)}) collective-permute-start(f32[4,256]{1,0:T(4,128)S(1)} %get-tuple-element.22), channel_id=1, source_target_pairs={{0,1},{1,0},{2,3},{3,2},{4,5},{5,4},{6,7},{7,6},{8,9},{9,8},{10,11... | collective-permute-start | bytes 12296 | tf_op jit(solution)/shard_map/ppermute | solution.py:184

commit v7 on v6

--- a/solution.py
+++ b/solution.py
@@ -20,7 +20,7 @@
 
 
 def owner_in_turn(owners, place):
-    return (place + owners // 2 + owners // 16) % owners
+    return (place + owners // 2 + owners // 16 + 1) % owners
 
 
 def pack_kernel(slot_ref, amp_ref, out_ref, slots_in, amp_in, slot_sem, amp_sem):

time: 74.5 us -> 74.4 us (level)
    all_to_all x1, starting transfers between devices: 20.1 us -> 19.2 us  [on_device(): lax.all_to_all(send, 'pair', split_axis=0, concat_axis=0, tiled=True, axi...]
where the time goes in v7:
time: 74.4 us; the launch traced here: 74 us
  starting transfers between devices  32 us (43%)
  blocking collectives  22.9 us (31%)
  waiting for transfers between devices  10.1 us (14%)
  Pallas kernels  3.89 us (5%)
  other arithmetic  2.62 us (4%)
  between operations  1.58 us (2%)
  local copies, waits for them, and re-layouts  0.96 us (1%)
    all_to_all x1, blocking collectives, on_device(): lax.all_to_all(partial, 'pair', split_axis=0, concat_axis=0, tiled=True,...  22.9 us
    all_to_all x1, starting transfers between devices, on_device(): lax.all_to_all(send, 'pair', split_axis=0, concat_axis=0, tiled=True, axi...  19.2 us
    ppermute x1, starting transfers between devices, on_device(): came = lax.ppermute(halves[half:], 'intg', swap)  5.25 us
    ppermute x1, waiting for transfers between devices, on_device(): other = lax.ppermute(piece, 'intg', ring)  5.01 us
    ppermute x1, starting transfers between devices, on_device(): other = lax.ppermute(piece, 'intg', ring)  4.38 us
    all_to_all x1, waiting for transfers between devices, on_device(): lax.all_to_all(send, 'pair', split_axis=0, concat_axis=0, tiled=True, axi...  4.33 us
    ppermute x1, starting transfers between devices, on_device(): other_ints = lax.ppermute(masked_ints, 'intg', swap)  3.14 us
    pallas_call x1, Pallas kernels, pack(): pl.pallas_call(pack_kernel, out_shape=jax.ShapeDtypeStruct((owners, SLOTS...  2.39 us
  transfers between devices with their start and end apart: 4, of which 3 were waited for; matrix products, arithmetic and copies ran while one was open for 4% of the time, Pallas kernels for 1%

profile of v7, /device:TPU:1, one launch (start us, length us, event | category | flops | bytes accessed | tf_op | source)
XLA Modules:
  0.0 74.0 jit_solution(4554708306248509558)
XLA Ops:
  0.0 0.0 copy-start.3
  0.0 0.0 copy-start
  0.0 0.0 copy-start.5
  0.0 0.0 copy-start.1
  0.0 2.4 %pack.1 = bf16[64,8,512]{2,1,0:T(8,128)(2,1)} custom-call(s32[1,128]{1,0:T(1,128)} %bitcast.12, bf16[8,128,1024]{2,1,0:T(8,128)(2,1)} %amp_ref.1), custom_call_target="tpu_custom_call" | custom-call | tf_op jit(solution)/shard_map/pack/pallas_call | solution.py:68
  2.4 0.0 copy-start.4
  2.4 0.0 copy-start.2
  2.4 19.2 %all-to-all-start = ((bf16[64,8,512]{2,1,0:T(8,128)(2,1)}), bf16[64,8,512]{2,1,0:T(8,128)(2,1)S(1)}, u32[]{:S(2)}, u32[]{:S(2)}) async-start(bf16[64,8,512]{2,1,0:T(8,128)(2,1)} %pack.1), calls=%async_computation | async-start | bytes 1048576 | tf_op jit(solution)/shard_map/all_to_all | solution.py:145
  21.7 0.0 copy-done.3
  21.7 0.1 and_select_fusion.1
  21.8 0.0 copy-done.5
  21.8 0.2 fusion.4
  22.0 0.0 copy-done.1
  22.0 0.2 fusion.3
  22.2 0.7 fusion.6
  24.3 0.0 copy-done
  24.3 0.3 fusion.mine_ref
  24.6 3.1 %collective-permute-start = (bf16[2,256,1024]{2,1,0:T(8,128)(2,1)S(1)}, bf16[2,256,1024]{2,1,0:T(8,128)(2,1)S(1)}, u32[]{:S(2)}, u32[]{:S(2)}) collective-permute-start(bf16[2,256,1024]{2,1,0:T(8,128)(2,1)S(1)} %fusion.mine_ref), channel_id=1, source_target_pairs={{0,1},{1,0},{2,3},{3,2},{4,5},{5,4},{6,7},{7,6},{8,9},{9,8},{10,11... | collective-permute-start | bytes 3145736 | tf_op jit(solution)/shard_map/ppermute | solution.py:163
  27.8 0.8 %fusion.10 = (f32[32]{0:T(128)S(1)}, f32[32]{0:T(128)S(1)}) fusion(f32[768]{0:T(1024)} %param.15, s32[]{:T(128)S(6)} %select_n.93, s32[]{:T(128)S(6)} %select_n.94), kind=kLoop, calls=%fused_computation.28 | loop fusion | bytes 520 | tf_op jit(solution)/shard_map/dynamic_slice | solution.py:171
  28.7 0.1 broadcast_add_fusion
  28.7 0.1 add.49
  28.8 4.3 %all-to-all-done = bf16[64,8,512]{2,1,0:T(8,128)(2,1)S(1)} async-done(((bf16[64,8,512]{2,1,0:T(8,128)(2,1)}), bf16[64,8,512]{2,1,0:T(8,128)(2,1)S(1)}, u32[]{:S(2)}, u32[]{:S(2)}) %all-to-all-start) | async-done | bytes 524320 | tf_op jit(solution)/shard_map/all_to_all | solution.py:145
  33.1 4.4 %collective-permute-start.1 = (bf16[512,512]{1,0:T(8,128)(2,1)S(1)}, bf16[512,512]{1,0:T(8,128)(2,1)S(1)}, u32[]{:S(2)}, u32[]{:S(2)}) collective-permute-start(bf16[512,512]{1,0:T(8,128)(2,1)S(1)} %bitcast.9), channel_id=1, source_target_pairs={{0,2},{1,7},{2,4},{3,1},{4,6},{5,3},{6,0},{7,5},{8,10},{9,15},{10,... | collective-permute-start | bytes 1572872 | tf_op jit(solution)/shard_map/ppermute | solution.py:166
  37.5 0.0 copy-done.4
  37.5 0.0 copy-done.2
  37.5 0.2 select_reduce_fusion
  37.8 0.1 broadcast_subtract_fusion
  37.8 0.0 collective-permute-done.theirs_ref
  37.8 0.7 %ladder.2.refs_0_ = f32[64,8,256]{2,1,0:T(8,128)S(1)} custom-call(bf16[2,256,1024]{2,1,0:T(8,128)(2,1)S(1)} %fusion.mine_ref, bf16[2,256,1024]{2,1,0:T(8,128)(2,1)S(1)} %collective-permute-done.theirs_ref, bf16[512,512]{1,0:T(8,128)(2,1)S(1)} %bitcast.10), custom_call_target="tpu_custom_call" | custom-call | tf_op jit(solution)/shard_map/ladder/pallas_call | solution.py:112
  38.6 5.0 %collective-permute-done.1.columns_ref = bf16[512,512]{1,0:T(8,128)(2,1)S(1)} collective-permute-done((bf16[512,512]{1,0:T(8,128)(2,1)S(1)}, bf16[512,512]{1,0:T(8,128)(2,1)S(1)}, u32[]{:S(2)}, u32[]{:S(2)}) %collective-permute-start.1) | collective-permute-done | bytes 524320 | tf_op jit(solution)/shard_map/ppermute | solution.py:166
  43.6 0.7 %ladder.3 = f32[64,8,256]{2,1,0:T(8,128)S(1)} custom-call(bf16[2,256,1024]{2,1,0:T(8,128)(2,1)S(1)} %fusion.mine_ref, bf16[2,256,1024]{2,1,0:T(8,128)(2,1)S(1)} %collective-permute-done.theirs_ref, bf16[512,512]{1,0:T(8,128)(2,1)S(1)} %collective-permute-done.1.columns_ref, f32[64,8,256]{2,1,0:T(8,128)S(1)} %ladder.2.refs_0_), custom_call_target="tpu_custom_call" | custom-call | tf_op jit(solution)/shard_map/ladder/pallas_call | solution.py:112
  44.4 22.9 %all_to_all.10 = f32[64,8,256]{2,1,0:T(8,128)S(1)} all-to-all(f32[64,8,256]{2,1,0:T(8,128)S(1)} %ladder.3), channel_id=1, replica_groups={{296,304,312,320,328,336,344,352,360,368,376,384,392,400,408,416,424,43..., dimensions={0} | all-to-all | bytes 1048576 | tf_op jit(solution)/shard_map/all_to_all | solution.py:181
  67.3 0.1 reduce_sum.79
  67.3 5.3 %collective-permute-start.2 = (f32[4,256]{1,0:T(4,128)S(1)}, f32[4,256]{1,0:T(4,128)S(1)}, u32[]{:S(2)}, u32[]{:S(2)}) collective-permute-start(f32[4,256]{1,0:T(4,128)S(1)} %get-tuple-element.22), channel_id=1, source_target_pairs={{0,1},{1,0},{2,3},{3,2},{4,5},{5,4},{6,7},{7,6},{8,9},{9,8},{10,11... | collective-permute-start | bytes 12296 | tf_op jit(solution)/shard_map/ppermute | solution.py:184
  72.6 0.8 %collective-permute-done.2 = f32[4,256]{1,0:T(4,128)S(1)} collective-permute-done((f32[4,256]{1,0:T(4,128)S(1)}, f32[4,256]{1,0:T(4,128)S(1)}, u32[]{:S(2)}, u32[]{:S(2)}) %collective-permute-start.2) | collective-permute-done | bytes 4128 | tf_op jit(solution)/shard_map/ppermute | solution.py:184
  73.4 0.6 fusion.1
  (5 shorter events, 0.0 us)
Async XLA Ops:
  0.0 21.7 %copy-start.3 = (s32[128]{0:T(128)S(1)}, s32[128]{0:T(128)}, u32[]{:S(2)}) copy-start(s32[128]{0:T(128)} %param.12) | copy-start | bytes 1540
  0.0 24.3 %copy-start = (bf16[256,2,1024]{2,1,0:T(2,128)(2,1)S(1)}, bf16[256,2,1024]{2,1,0:T(2,128)(2,1)}, u32[]{:S(2)}) copy-start(bf16[256,2,1024]{2,1,0:T(2,128)(2,1)} %param.9) | copy-start | bytes 3145732
  0.0 21.8 %copy-start.5 = (s32[128]{0:T(128)S(1)}, s32[128]{0:T(128)}, u32[]{:S(2)}) copy-start(s32[128]{0:T(128)} %param.11) | copy-start | bytes 1540
  0.0 22.0 %copy-start.1 = (s32[24]{0:T(128)S(1)}, s32[24]{0:T(128)}, u32[]{:S(2)}) copy-start(s32[24]{0:T(128)} %param.10) | copy-start | bytes 292
  2.4 35.1 %copy-start.4 = (s32[8,2]{0,1:T(2,128)S(1)}, s32[8,2]{0,1:T(2,128)}, u32[]{:S(2)}) copy-start(s32[8,2]{0,1:T(2,128)} %param.13) | copy-start | bytes 196
  2.4 35.1 %copy-start.2 = (f32[300]{0:T(512)S(1)}, f32[300]{0:T(512)}, u32[]{:S(2)}) copy-start(f32[300]{0:T(512)} %param.14) | copy-start | bytes 3604
  2.4 30.7 %all-to-all-start = ((bf16[64,8,512]{2,1,0:T(8,128)(2,1)}), bf16[64,8,512]{2,1,0:T(8,128)(2,1)S(1)}, u32[]{:S(2)}, u32[]{:S(2)}) async-start(bf16[64,8,512]{2,1,0:T(8,128)(2,1)} %pack.1), calls=%async_computation | async-start | bytes 1048576 | tf_op jit(solution)/shard_map/all_to_all | solution.py:145
  24.6 13.2 %collective-permute-start = (bf16[2,256,1024]{2,1,0:T(8,128)(2,1)S(1)}, bf16[2,256,1024]{2,1,0:T(8,128)(2,1)S(1)}, u32[]{:S(2)}, u32[]{:S(2)}) collective-permute-start(bf16[2,256,1024]{2,1,0:T(8,128)(2,1)S(1)} %fusion.mine_ref), channel_id=1, source_target_pairs={{0,1},{1,0},{2,3},{3,2},{4,5},{5,4},{6,7},{7,6},{8,9},{9,8},{10,11... | collective-permute-start | bytes 3145736 | tf_op jit(solution)/shard_map/ppermute | solution.py:163
  33.1 10.5 %collective-permute-start.1 = (bf16[512,512]{1,0:T(8,128)(2,1)S(1)}, bf16[512,512]{1,0:T(8,128)(2,1)S(1)}, u32[]{:S(2)}, u32[]{:S(2)}) collective-permute-start(bf16[512,512]{1,0:T(8,128)(2,1)S(1)} %bitcast.9), channel_id=1, source_target_pairs={{0,2},{1,7},{2,4},{3,1},{4,6},{5,3},{6,0},{7,5},{8,10},{9,15},{10,... | collective-permute-start | bytes 1572872 | tf_op jit(solution)/shard_map/ppermute | solution.py:166
  67.3 6.1 %collective-permute-start.2 = (f32[4,256]{1,0:T(4,128)S(1)}, f32[4,256]{1,0:T(4,128)S(1)}, u32[]{:S(2)}, u32[]{:S(2)}) collective-permute-start(f32[4,256]{1,0:T(4,128)S(1)} %get-tuple-element.22), channel_id=1, source_target_pairs={{0,1},{1,0},{2,3},{3,2},{4,5},{5,4},{6,7},{7,6},{8,9},{9,8},{10,11... | collective-permute-start | bytes 12296 | tf_op jit(solution)/shard_map/ppermute | solution.py:184

commit v8 on v7

--- a/solution.py
+++ b/solution.py
@@ -181,7 +181,7 @@
     parts = lax.all_to_all(partial, "pair", split_axis=0, concat_axis=0, tiled=True, axis_index_groups=in_turn)
     halves = jnp.sum(parts, axis=0)
     kept = halves[:half]
-    came = lax.ppermute(halves[half:], "intg", swap)
+    came = lax.ppermute(halves, "intg", swap)[half:]
     ladder = jnp.where(
         block % CORES == 0, jnp.concatenate([kept, came]), jnp.concatenate([came, kept])
     )

time: 74.4 us -> 74.4 us (level)
  no operation moved by 1% of the time
where the time goes in v8:
time: 74.4 us; the launch traced here: 74 us
  starting transfers between devices  32 us (43%)
  blocking collectives  22.9 us (31%)
  waiting for transfers between devices  10.1 us (14%)
  Pallas kernels  3.89 us (5%)
  other arithmetic  2.62 us (4%)
  between operations  1.58 us (2%)
  local copies, waits for them, and re-layouts  0.96 us (1%)
    all_to_all x1, blocking collectives, on_device(): lax.all_to_all(partial, 'pair', split_axis=0, concat_axis=0, tiled=True,...  22.9 us
    all_to_all x1, starting transfers between devices, on_device(): lax.all_to_all(send, 'pair', split_axis=0, concat_axis=0, tiled=True, axi...  19.2 us
    ppermute x1, starting transfers between devices, on_device(): came = lax.ppermute(halves, 'intg', swap)[half:]  5.25 us
    ppermute x1, waiting for transfers between devices, on_device(): other = lax.ppermute(piece, 'intg', ring)  5.01 us
    ppermute x1, starting transfers between devices, on_device(): other = lax.ppermute(piece, 'intg', ring)  4.38 us
    all_to_all x1, waiting for transfers between devices, on_device(): lax.all_to_all(send, 'pair', split_axis=0, concat_axis=0, tiled=True, axi...  4.33 us
    ppermute x1, starting transfers between devices, on_device(): other_ints = lax.ppermute(masked_ints, 'intg', swap)  3.14 us
    pallas_call x1, Pallas kernels, pack(): pl.pallas_call(pack_kernel, out_shape=jax.ShapeDtypeStruct((owners, SLOTS...  2.39 us
  transfers between devices with their start and end apart: 4, of which 3 were waited for; matrix products, arithmetic and copies ran while one was open for 4% of the time, Pallas kernels for 1%

profile of v8, /device:TPU:1, one launch (start us, length us, event | category | flops | bytes accessed | tf_op | source)
XLA Modules:
  0.0 74.0 jit_solution(9200509646606900882)
XLA Ops:
  0.0 0.0 copy-start.3
  0.0 0.0 copy-start
  0.0 0.0 copy-start.5
  0.0 0.0 copy-start.1
  0.0 2.4 %pack.1 = bf16[64,8,512]{2,1,0:T(8,128)(2,1)} custom-call(s32[1,128]{1,0:T(1,128)} %bitcast.12, bf16[8,128,1024]{2,1,0:T(8,128)(2,1)} %amp_ref.1), custom_call_target="tpu_custom_call" | custom-call | tf_op jit(solution)/shard_map/pack/pallas_call | solution.py:68
  2.4 0.0 copy-start.4
  2.4 0.0 copy-start.2
  2.4 19.2 %all-to-all-start = ((bf16[64,8,512]{2,1,0:T(8,128)(2,1)}), bf16[64,8,512]{2,1,0:T(8,128)(2,1)S(1)}, u32[]{:S(2)}, u32[]{:S(2)}) async-start(bf16[64,8,512]{2,1,0:T(8,128)(2,1)} %pack.1), calls=%async_computation | async-start | bytes 1048576 | tf_op jit(solution)/shard_map/all_to_all | solution.py:145
  21.7 0.0 copy-done.3
  21.7 0.1 and_select_fusion.1
  21.8 0.0 copy-done.5
  21.8 0.2 fusion.4
  22.0 0.0 copy-done.1
  22.0 0.2 fusion.3
  22.2 0.7 fusion.6
  24.3 0.0 copy-done
  24.3 0.3 fusion.mine_ref
  24.6 3.1 %collective-permute-start = (bf16[2,256,1024]{2,1,0:T(8,128)(2,1)S(1)}, bf16[2,256,1024]{2,1,0:T(8,128)(2,1)S(1)}, u32[]{:S(2)}, u32[]{:S(2)}) collective-permute-start(bf16[2,256,1024]{2,1,0:T(8,128)(2,1)S(1)} %fusion.mine_ref), channel_id=1, source_target_pairs={{0,1},{1,0},{2,3},{3,2},{4,5},{5,4},{6,7},{7,6},{8,9},{9,8},{10,11... | collective-permute-start | bytes 3145736 | tf_op jit(solution)/shard_map/ppermute | solution.py:163
  27.8 0.8 %fusion.9 = (f32[32]{0:T(128)S(1)}, f32[32]{0:T(128)S(1)}) fusion(f32[768]{0:T(1024)} %param.15, s32[]{:T(128)S(6)} %select_n.93, s32[]{:T(128)S(6)} %select_n.94), kind=kLoop, calls=%fused_computation.27 | loop fusion | bytes 520 | tf_op jit(solution)/shard_map/dynamic_slice | solution.py:171
  28.7 0.1 broadcast_add_fusion
  28.7 0.1 add.49
  28.8 4.3 %all-to-all-done = bf16[64,8,512]{2,1,0:T(8,128)(2,1)S(1)} async-done(((bf16[64,8,512]{2,1,0:T(8,128)(2,1)}), bf16[64,8,512]{2,1,0:T(8,128)(2,1)S(1)}, u32[]{:S(2)}, u32[]{:S(2)}) %all-to-all-start) | async-done | bytes 524320 | tf_op jit(solution)/shard_map/all_to_all | solution.py:145
  33.1 4.4 %collective-permute-start.1 = (bf16[512,512]{1,0:T(8,128)(2,1)S(1)}, bf16[512,512]{1,0:T(8,128)(2,1)S(1)}, u32[]{:S(2)}, u32[]{:S(2)}) collective-permute-start(bf16[512,512]{1,0:T(8,128)(2,1)S(1)} %bitcast.9), channel_id=1, source_target_pairs={{0,2},{1,7},{2,4},{3,1},{4,6},{5,3},{6,0},{7,5},{8,10},{9,15},{10,... | collective-permute-start | bytes 1572872 | tf_op jit(solution)/shard_map/ppermute | solution.py:166
  37.5 0.0 copy-done.4
  37.5 0.0 copy-done.2
  37.5 0.2 select_reduce_fusion
  37.8 0.1 broadcast_subtract_fusion
  37.8 0.0 collective-permute-done.theirs_ref
  37.8 0.7 %ladder.2.refs_0_ = f32[64,8,256]{2,1,0:T(8,128)S(1)} custom-call(bf16[2,256,1024]{2,1,0:T(8,128)(2,1)S(1)} %fusion.mine_ref, bf16[2,256,1024]{2,1,0:T(8,128)(2,1)S(1)} %collective-permute-done.theirs_ref, bf16[512,512]{1,0:T(8,128)(2,1)S(1)} %bitcast.10), custom_call_target="tpu_custom_call" | custom-call | tf_op jit(solution)/shard_map/ladder/pallas_call | solution.py:112
  38.6 5.0 %collective-permute-done.1.columns_ref = bf16[512,512]{1,0:T(8,128)(2,1)S(1)} collective-permute-done((bf16[512,512]{1,0:T(8,128)(2,1)S(1)}, bf16[512,512]{1,0:T(8,128)(2,1)S(1)}, u32[]{:S(2)}, u32[]{:S(2)}) %collective-permute-start.1) | collective-permute-done | bytes 524320 | tf_op jit(solution)/shard_map/ppermute | solution.py:166
  43.6 0.7 %ladder.3 = f32[64,8,256]{2,1,0:T(8,128)S(1)} custom-call(bf16[2,256,1024]{2,1,0:T(8,128)(2,1)S(1)} %fusion.mine_ref, bf16[2,256,1024]{2,1,0:T(8,128)(2,1)S(1)} %collective-permute-done.theirs_ref, bf16[512,512]{1,0:T(8,128)(2,1)S(1)} %collective-permute-done.1.columns_ref, f32[64,8,256]{2,1,0:T(8,128)S(1)} %ladder.2.refs_0_), custom_call_target="tpu_custom_call" | custom-call | tf_op jit(solution)/shard_map/ladder/pallas_call | solution.py:112
  44.4 22.9 %all_to_all.10 = f32[64,8,256]{2,1,0:T(8,128)S(1)} all-to-all(f32[64,8,256]{2,1,0:T(8,128)S(1)} %ladder.3), channel_id=1, replica_groups={{296,304,312,320,328,336,344,352,360,368,376,384,392,400,408,416,424,43..., dimensions={0} | all-to-all | bytes 1048576 | tf_op jit(solution)/shard_map/all_to_all | solution.py:181
  67.3 0.1 reduce_sum.79
  67.3 5.3 %collective-permute-start.2 = (f32[8,256]{1,0:T(8,128)S(1)}, f32[8,256]{1,0:T(8,128)S(1)}, u32[]{:S(2)}, u32[]{:S(2)}) collective-permute-start(f32[8,256]{1,0:T(8,128)S(1)} %reduce_sum.79), channel_id=1, source_target_pairs={{0,1},{1,0},{2,3},{3,2},{4,5},{5,4},{6,7},{7,6},{8,9},{9,8},{10,11... | collective-permute-start | bytes 24584 | tf_op jit(solution)/shard_map/ppermute | solution.py:184
  72.6 0.8 %collective-permute-done.2 = f32[8,256]{1,0:T(8,128)S(1)} collective-permute-done((f32[8,256]{1,0:T(8,128)S(1)}, f32[8,256]{1,0:T(8,128)S(1)}, u32[]{:S(2)}, u32[]{:S(2)}) %collective-permute-start.2) | collective-permute-done | bytes 8224 | tf_op jit(solution)/shard_map/ppermute | solution.py:184
  73.4 0.6 fusion.1
  (6 shorter events, 0.0 us)
Async XLA Ops:
  0.0 21.7 %copy-start.3 = (s32[128]{0:T(128)S(1)}, s32[128]{0:T(128)}, u32[]{:S(2)}) copy-start(s32[128]{0:T(128)} %param.12) | copy-start | bytes 1540
  0.0 24.3 %copy-start = (bf16[256,2,1024]{2,1,0:T(2,128)(2,1)S(1)}, bf16[256,2,1024]{2,1,0:T(2,128)(2,1)}, u32[]{:S(2)}) copy-start(bf16[256,2,1024]{2,1,0:T(2,128)(2,1)} %param.9) | copy-start | bytes 3145732
  0.0 21.8 %copy-start.5 = (s32[128]{0:T(128)S(1)}, s32[128]{0:T(128)}, u32[]{:S(2)}) copy-start(s32[128]{0:T(128)} %param.11) | copy-start | bytes 1540
  0.0 22.0 %copy-start.1 = (s32[24]{0:T(128)S(1)}, s32[24]{0:T(128)}, u32[]{:S(2)}) copy-start(s32[24]{0:T(128)} %param.10) | copy-start | bytes 292
  2.4 35.1 %copy-start.4 = (s32[8,2]{0,1:T(2,128)S(1)}, s32[8,2]{0,1:T(2,128)}, u32[]{:S(2)}) copy-start(s32[8,2]{0,1:T(2,128)} %param.13) | copy-start | bytes 196
  2.4 35.1 %copy-start.2 = (f32[300]{0:T(512)S(1)}, f32[300]{0:T(512)}, u32[]{:S(2)}) copy-start(f32[300]{0:T(512)} %param.14) | copy-start | bytes 3604
  2.4 30.7 %all-to-all-start = ((bf16[64,8,512]{2,1,0:T(8,128)(2,1)}), bf16[64,8,512]{2,1,0:T(8,128)(2,1)S(1)}, u32[]{:S(2)}, u32[]{:S(2)}) async-start(bf16[64,8,512]{2,1,0:T(8,128)(2,1)} %pack.1), calls=%async_computation | async-start | bytes 1048576 | tf_op jit(solution)/shard_map/all_to_all | solution.py:145
  24.6 13.2 %collective-permute-start = (bf16[2,256,1024]{2,1,0:T(8,128)(2,1)S(1)}, bf16[2,256,1024]{2,1,0:T(8,128)(2,1)S(1)}, u32[]{:S(2)}, u32[]{:S(2)}) collective-permute-start(bf16[2,256,1024]{2,1,0:T(8,128)(2,1)S(1)} %fusion.mine_ref), channel_id=1, source_target_pairs={{0,1},{1,0},{2,3},{3,2},{4,5},{5,4},{6,7},{7,6},{8,9},{9,8},{10,11... | collective-permute-start | bytes 3145736 | tf_op jit(solution)/shard_map/ppermute | solution.py:163
  33.1 10.5 %collective-permute-start.1 = (bf16[512,512]{1,0:T(8,128)(2,1)S(1)}, bf16[512,512]{1,0:T(8,128)(2,1)S(1)}, u32[]{:S(2)}, u32[]{:S(2)}) collective-permute-start(bf16[512,512]{1,0:T(8,128)(2,1)S(1)} %bitcast.9), channel_id=1, source_target_pairs={{0,2},{1,7},{2,4},{3,1},{4,6},{5,3},{6,0},{7,5},{8,10},{9,15},{10,... | collective-permute-start | bytes 1572872 | tf_op jit(solution)/shard_map/ppermute | solution.py:166
  67.3 6.1 %collective-permute-start.2 = (f32[8,256]{1,0:T(8,128)S(1)}, f32[8,256]{1,0:T(8,128)S(1)}, u32[]{:S(2)}, u32[]{:S(2)}) collective-permute-start(f32[8,256]{1,0:T(8,128)S(1)} %reduce_sum.79), channel_id=1, source_target_pairs={{0,1},{1,0},{2,3},{3,2},{4,5},{5,4},{6,7},{7,6},{8,9},{9,8},{10,11... | collective-permute-start | bytes 24584 | tf_op jit(solution)/shard_map/ppermute | solution.py:184
